TPU v7x, 512 devices: a whole 4x8x8 slice. The times are simulated.
512 devices in a mesh: mode: 32 (over y, x), elem: 16 (over z, core).
Axes of the slice: x: 4, y: 8, z: 8, core: 2. Of those that a mesh axis runs over, the one named last changes fastest.
Arguments:
- rhs_phys: float32 [512, 49152], P(None, ('elem', 'mode')), may hold values from -6 to 6
- radial_basis: float32 [48, 128, 128], P('elem'), may hold values from -0.5 to 0.5
- axial_basis: float32 [48, 7, 7], P('elem'), may hold values from -2 to 2
- radial_eig: float32 [48, 128], P('elem'), may hold values from 0.25 to 8
- axial_eig: float32 [48, 7], P('elem'), may hold values from 0.25 to 8
- face_stiff: float32 [48, 128, 128], P('elem'), may hold values from -0.5 to 0.5
- face_mass: float32 [48, 128, 128], P('elem'), may hold values from -0.5 to 0.5
- axial_coupling: float32 [48, 2, 7], P('elem'), may hold values from -3 to 3
- face_numbering: int32 [48, 2, 128], P('elem'), may hold values from 0 to 127, each once within a row
- band_panels: float32 [2, 48, 128, 128], P(None, 'elem'), may hold values from -1 to 1
- inverse_panels: float32 [256, 48, 128, 128], P('mode', 'elem'), may hold values from -2 to 2
Outputs:
- pressure: float32 [512, 49152], P('mode', 'elem')
Inputs may be any that keep to these rules, and one draw needn't show every extreme that they name: Each row of face_numbering is a permutation of 0 to 127.
All inputs are finite; a program needn't handle non-finite values.
Results may differ from a plain program's by a relative error of at most 0.0003.
Values sent between devices are 32-bit elements; how exact they have to be, the bound alone decides.
A program may use at most 64 MiB of HBM per device.

v0:
```python
import math

import jax
import jax.numpy as jnp
from jax import lax
from jax.sharding import PartitionSpec as P

HIGHEST = lax.Precision.HIGHEST


def shifted(block, axis, distance):
    devices = range(lax.axis_size(axis))
    route = [(i - distance, i) for i in devices if i - distance in devices]
    return lax.ppermute(block, axis, route)


def inverse_interior(values, radial_basis, axial_basis, denominator):
    section_one = jnp.einsum("mcjar,jrs->mcjas", values, radial_basis, precision=HIGHEST)
    section_one = jnp.einsum("mcjas,jab->mcjbs", section_one, axial_basis, precision=HIGHEST)
    section_one = section_one / denominator[:, None]
    section_one = jnp.einsum("mcjbs,jrs->mcjbr", section_one, radial_basis, precision=HIGHEST)
    return jnp.einsum("mcjbr,jab->mcjar", section_one, axial_basis, precision=HIGHEST)


def apply_panel(matrix, vector):
    return jnp.einsum("mrs,mcs->mcr", matrix, vector, precision=HIGHEST)


def apply_transposed(matrix, vector):
    return jnp.einsum("mrs,mcr->mcs", matrix, vector, precision=HIGHEST)


def body(
    rhs_phys,
    radial_basis,
    axial_basis,
    radial_eig,
    axial_eig,
    face_stiff,
    face_mass,
    axial_coupling,
    face_numbering,
    band_panels,
    inverse_panels,
):
    planes = rhs_phys.shape[0]
    mode_dev = inverse_panels.shape[0]
    slab_dev = inverse_panels.shape[1]
    radial = inverse_panels.shape[2]
    inner_count = axial_basis.shape[1]
    mode_total = mode_dev * lax.axis_size("mode")
    row_index = lax.broadcasted_iota(jnp.int32, (planes, planes), 0)
    col_index = lax.broadcasted_iota(jnp.int32, (planes, planes), 1)
    phase_index = row_index // 2 * col_index % planes
    angles = phase_index.astype(jnp.float32) * (2.0 * math.pi / planes)
    dft_table = jnp.where(row_index % 2 == 0, jnp.cos(angles), -jnp.sin(angles)) / math.sqrt(planes)
    spectrum = jnp.dot(dft_table, rhs_phys, precision=HIGHEST, preferred_element_type=jnp.float32)
    spectrum = lax.all_to_all(spectrum, "mode", split_axis=0, concat_axis=1, tiled=True)
    fields = spectrum.reshape(mode_dev, 2, slab_dev, inner_count + 1, radial)
    source_in = fields[:, :, :, :inner_count]
    source_bd = fields[:, :, :, inner_count]
    wavenumber = (lax.axis_index("mode") * mode_dev + jnp.arange(mode_dev, dtype=jnp.int32)).astype(
        jnp.float32
    ) / mode_total
    wavenumber_squared = 4.0 * wavenumber * wavenumber
    denominator = (
        axial_eig[None, :, :, None]
        + radial_eig[None, :, None, :]
        + wavenumber_squared[:, None, None, None]
    )
    solved_values = inverse_interior(source_in, radial_basis, axial_basis, denominator)
    onehot = (face_numbering[..., None] == jnp.arange(radial, dtype=jnp.int32)).astype(jnp.float32)
    wave_five = wavenumber_squared[:, None, None, None, None]
    face_sums = jnp.einsum("mcjar,jsa->mcjsr", solved_values, axial_coupling, precision=HIGHEST)
    pushed = jnp.einsum(
        "mcjsr,jrq->mcjsq", face_sums, face_stiff, precision=HIGHEST
    ) + wave_five * jnp.einsum("mcjsr,jrq->mcjsq", face_sums, face_mass, precision=HIGHEST)
    placed = jnp.einsum("mcjsq,jsqp->mcjsp", pushed, onehot, precision=HIGHEST)
    incoming = shifted(placed[:, :, 0, 0], "elem", -1)
    from_right = jnp.concatenate([placed[:, :, 1:, 0], incoming[:, :, None]], axis=2)
    reduced = source_bd - placed[:, :, :, 1] - from_right
    coupling = band_panels[0][None] + wavenumber_squared[:, None, None, None] * band_panels[1][None]
    zero_vec = jnp.zeros((mode_dev, 2, radial), jnp.float32)
    identity_mat = jnp.broadcast_to(jnp.eye(radial, dtype=jnp.float32), (mode_dev, radial, radial))

    def forward(start_vec):
        output_values = []
        current = start_vec
        for slab_index in range(slab_dev):
            inner_term = reduced[:, :, slab_index] - apply_panel(coupling[:, slab_index], current)
            current = apply_panel(inverse_panels[:, slab_index], inner_term)
            output_values.append(current)
        return output_values

    def backward(start_vec, forward_vals):
        output_values = [None] * slab_dev
        current = start_vec
        for slab_index in reversed(range(slab_dev)):
            solution = forward_vals[slab_index] - apply_panel(
                inverse_panels[:, slab_index], current
            )
            output_values[slab_index] = solution
            current = apply_transposed(coupling[:, slab_index], solution)
        return (output_values, current)

    forward_map = identity_mat
    for slab_index in range(slab_dev):
        banded = jnp.einsum("mrs,mst->mrt", coupling[:, slab_index], forward_map, precision=HIGHEST)
        forward_map = -jnp.einsum(
            "mrs,mst->mrt", inverse_panels[:, slab_index], banded, precision=HIGHEST
        )
    forward_offset = forward(zero_vec)[-1]

    def forward_round(turn_index, carried):
        return shifted(apply_panel(forward_map, carried) + forward_offset, "elem", 1)

    forward_start = lax.fori_loop(0, lax.axis_size("elem") - 1, forward_round, zero_vec)
    forward_vals = forward(forward_start)
    backward_map = identity_mat
    for slab_index in reversed(range(slab_dev)):
        solved_map = jnp.einsum(
            "mrs,mst->mrt", inverse_panels[:, slab_index], backward_map, precision=HIGHEST
        )
        backward_map = -jnp.einsum(
            "mrs,mrt->mst", coupling[:, slab_index], solved_map, precision=HIGHEST
        )
    backward_offset = backward(zero_vec, forward_vals)[1]

    def backward_round(turn_index, carried):
        return shifted(apply_panel(backward_map, carried) + backward_offset, "elem", -1)

    backward_start = lax.fori_loop(0, lax.axis_size("elem") - 1, backward_round, zero_vec)
    back_vals = backward(backward_start, forward_vals)[0]
    interface = jnp.stack(back_vals, axis=2)
    before = shifted(interface[:, :, -1], "elem", 1)
    previous = jnp.concatenate([before[:, :, None], interface[:, :, :-1]], axis=2)
    face_vals = jnp.stack([previous, interface], axis=3)
    local_face = jnp.einsum("mcjsp,jsqp->mcjsq", face_vals, onehot, precision=HIGHEST)
    lifted = jnp.einsum(
        "jrq,mcjsq->mcjsr", face_stiff, local_face, precision=HIGHEST
    ) + wave_five * jnp.einsum("jrq,mcjsq->mcjsr", face_mass, local_face, precision=HIGHEST)
    spread = jnp.einsum("mcjsr,jsa->mcjar", lifted, axial_coupling, precision=HIGHEST)
    interior_values = solved_values - inverse_interior(
        spread, radial_basis, axial_basis, denominator
    )
    assembled = jnp.concatenate([interior_values, interface[:, :, :, None]], axis=3)
    return assembled.reshape(2 * mode_dev, slab_dev * (inner_count + 1) * radial)


def solution(mesh):
    placed = (
        P(None, ("elem", "mode")),
        P("elem", None, None),
        P("elem", None, None),
        P("elem", None),
        P("elem", None),
        P("elem", None, None),
        P("elem", None, None),
        P("elem", None, None),
        P("elem", None, None),
        P(None, "elem", None, None),
        P("mode", "elem", None, None),
    )
    return jax.shard_map(
        body, mesh=mesh, in_specs=placed, out_specs=P("mode", "elem"), check_vma=False
    )
```

profile of v0, /device:TPU:195, one launch (start us, length us, event | category | flops | bytes accessed | tf_op | source)
XLA Modules:
  0.0 349.7 jit_solution(13140070393714998365)
XLA Ops:
  0.0 7.4 %fusion.12 = f32[512,96]{1,0:T(8,128)} fusion(f32[512,96]{0,1:T(8,128)} %param.15, s32[512]{0:T(512)S(1)} %get-tuple-element.75, s32[512]{0:T(512)S(1)} %get-tuple-element.78, s32[512]{0:T(512)S(1)} %get-tuple-element.76, s32[512]{0:T(512)S(1)} %get-tuple-element.77, pred[512]{0:T(512)(128)(4,1)S(1)} %get-tuple-element.79, ...), kind=kOutput, calls=%fused_computation.44 | convolution fusion | flops 307232768 | bytes 402432 | tf_op jit(solution)/shard_map/dot_general | solution.py:57
  7.4 9.9 %all-to-all-start = ((f32[32,16,96]{2,1,0:T(8,128)}), f32[32,16,96]{2,1,0:T(8,128)}, u32[]{:S(2)}, u32[]{:S(2)}) async-start(f32[32,16,96]{2,1,0:T(8,128)} %bitcast), calls=%async_computation | async-start | bytes 524288 | tf_op jit(solution)/shard_map/all_to_all | solution.py:58
  49.3 3.1 collective-permute-start.2
  53.5 3.5 %collective-permute-done.2 = f32[8,2,128]{2,0,1:T(8,128)S(1)} collective-permute-done((f32[8,2,128]{2,0,1:T(8,128)S(1)}, f32[8,2,128]{2,0,1:T(8,128)S(1)}, u32[]{:S(2)}, u32[]{:S(2)}) %collective-permute-start.2) | collective-permute-done | bytes 8224 | tf_op jit(solution)/shard_map/ppermute | solution.py:14
  61.7 130.8 %while.20 = (s32[]{:T(128)}, f32[8,2,128]{2,1,0:T(2,128)S(1)}, f32[8,128,128]{2,1,0:T(8,128)}, f32[8,2,128]{2,1,0:T(2,128)S(1)}, s32[]{:T(128)}) while((s32[]{:T(128)}, f32[8,2,128]{2,1,0:T(2,128)S(1)}, f32[8,128,128]{2,1,0:T(8,128)}, f32[8,2,128]{2,1,0:T(2,128)S(1)}, s32[]{:T(128)}) %tuple.37), condition=%wide.region_1.2_spmd, body=%wide.region_0.1_spmd.sunk | while | flops 3147778 | bytes 581733 | solution.py:117
  61.7 2.6 convolution_add_fusion.4
  67.6 2.6 convolution_add_fusion.4
  70.2 5.0 %collective-permute-start = (f32[8,2,128]{2,1,0:T(2,128)}, f32[8,2,128]{2,1,0:T(2,128)S(1)}, u32[]{:S(2)}, u32[]{:S(2)}) collective-permute-start(f32[8,2,128]{2,1,0:T(2,128)} %convolution_add_fusion.4), channel_id=1, source_target_pairs={{0,1},{1,2},{2,3},{3,4},{4,5},{5,6},{6,7},{7,8},{8,9},{9,10},{10,1... | collective-permute-start | bytes 24584 | tf_op jit(solution)/shard_map/while/body/eval_jaxpr/ppermute | solution.py:14
  76.2 2.6 convolution_add_fusion.4
  78.8 5.4 %collective-permute-start = (f32[8,2,128]{2,1,0:T(2,128)}, f32[8,2,128]{2,1,0:T(2,128)S(1)}, u32[]{:S(2)}, u32[]{:S(2)}) collective-permute-start(f32[8,2,128]{2,1,0:T(2,128)} %convolution_add_fusion.4), channel_id=1, source_target_pairs={{0,1},{1,2},{2,3},{3,4},{4,5},{5,6},{6,7},{7,8},{8,9},{9,10},{10,1... | collective-permute-start | bytes 24584 | tf_op jit(solution)/shard_map/while/body/eval_jaxpr/ppermute | solution.py:14
  85.1 2.6 convolution_add_fusion.4
  87.7 5.4 %collective-permute-start = (f32[8,2,128]{2,1,0:T(2,128)}, f32[8,2,128]{2,1,0:T(2,128)S(1)}, u32[]{:S(2)}, u32[]{:S(2)}) collective-permute-start(f32[8,2,128]{2,1,0:T(2,128)} %convolution_add_fusion.4), channel_id=1, source_target_pairs={{0,1},{1,2},{2,3},{3,4},{4,5},{5,6},{6,7},{7,8},{8,9},{9,10},{10,1... | collective-permute-start | bytes 24584 | tf_op jit(solution)/shard_map/while/body/eval_jaxpr/ppermute | solution.py:14
  94.1 2.6 convolution_add_fusion.4
  96.7 5.4 %collective-permute-start = (f32[8,2,128]{2,1,0:T(2,128)}, f32[8,2,128]{2,1,0:T(2,128)S(1)}, u32[]{:S(2)}, u32[]{:S(2)}) collective-permute-start(f32[8,2,128]{2,1,0:T(2,128)} %convolution_add_fusion.4), channel_id=1, source_target_pairs={{0,1},{1,2},{2,3},{3,4},{4,5},{5,6},{6,7},{7,8},{8,9},{9,10},{10,1... | collective-permute-start | bytes 24584 | tf_op jit(solution)/shard_map/while/body/eval_jaxpr/ppermute | solution.py:14
  103.0 2.6 convolution_add_fusion.4
  105.6 5.4 %collective-permute-start = (f32[8,2,128]{2,1,0:T(2,128)}, f32[8,2,128]{2,1,0:T(2,128)S(1)}, u32[]{:S(2)}, u32[]{:S(2)}) collective-permute-start(f32[8,2,128]{2,1,0:T(2,128)} %convolution_add_fusion.4), channel_id=1, source_target_pairs={{0,1},{1,2},{2,3},{3,4},{4,5},{5,6},{6,7},{7,8},{8,9},{9,10},{10,1... | collective-permute-start | bytes 24584 | tf_op jit(solution)/shard_map/while/body/eval_jaxpr/ppermute | solution.py:14
  112.0 2.6 convolution_add_fusion.4
  114.5 5.4 %collective-permute-start = (f32[8,2,128]{2,1,0:T(2,128)}, f32[8,2,128]{2,1,0:T(2,128)S(1)}, u32[]{:S(2)}, u32[]{:S(2)}) collective-permute-start(f32[8,2,128]{2,1,0:T(2,128)} %convolution_add_fusion.4), channel_id=1, source_target_pairs={{0,1},{1,2},{2,3},{3,4},{4,5},{5,6},{6,7},{7,8},{8,9},{9,10},{10,1... | collective-permute-start | bytes 24584 | tf_op jit(solution)/shard_map/while/body/eval_jaxpr/ppermute | solution.py:14
  120.9 2.6 convolution_add_fusion.4
  123.5 5.4 %collective-permute-start = (f32[8,2,128]{2,1,0:T(2,128)}, f32[8,2,128]{2,1,0:T(2,128)S(1)}, u32[]{:S(2)}, u32[]{:S(2)}) collective-permute-start(f32[8,2,128]{2,1,0:T(2,128)} %convolution_add_fusion.4), channel_id=1, source_target_pairs={{0,1},{1,2},{2,3},{3,4},{4,5},{5,6},{6,7},{7,8},{8,9},{9,10},{10,1... | collective-permute-start | bytes 24584 | tf_op jit(solution)/shard_map/while/body/eval_jaxpr/ppermute | solution.py:14
  129.9 2.6 convolution_add_fusion.4
  132.4 5.4 %collective-permute-start = (f32[8,2,128]{2,1,0:T(2,128)}, f32[8,2,128]{2,1,0:T(2,128)S(1)}, u32[]{:S(2)}, u32[]{:S(2)}) collective-permute-start(f32[8,2,128]{2,1,0:T(2,128)} %convolution_add_fusion.4), channel_id=1, source_target_pairs={{0,1},{1,2},{2,3},{3,4},{4,5},{5,6},{6,7},{7,8},{8,9},{9,10},{10,1... | collective-permute-start | bytes 24584 | tf_op jit(solution)/shard_map/while/body/eval_jaxpr/ppermute | solution.py:14
  138.8 2.6 convolution_add_fusion.4
  141.4 5.4 %collective-permute-start = (f32[8,2,128]{2,1,0:T(2,128)}, f32[8,2,128]{2,1,0:T(2,128)S(1)}, u32[]{:S(2)}, u32[]{:S(2)}) collective-permute-start(f32[8,2,128]{2,1,0:T(2,128)} %convolution_add_fusion.4), channel_id=1, source_target_pairs={{0,1},{1,2},{2,3},{3,4},{4,5},{5,6},{6,7},{7,8},{8,9},{9,10},{10,1... | collective-permute-start | bytes 24584 | tf_op jit(solution)/shard_map/while/body/eval_jaxpr/ppermute | solution.py:14
  147.8 2.6 convolution_add_fusion.4
  150.3 5.4 %collective-permute-start = (f32[8,2,128]{2,1,0:T(2,128)}, f32[8,2,128]{2,1,0:T(2,128)S(1)}, u32[]{:S(2)}, u32[]{:S(2)}) collective-permute-start(f32[8,2,128]{2,1,0:T(2,128)} %convolution_add_fusion.4), channel_id=1, source_target_pairs={{0,1},{1,2},{2,3},{3,4},{4,5},{5,6},{6,7},{7,8},{8,9},{9,10},{10,1... | collective-permute-start | bytes 24584 | tf_op jit(solution)/shard_map/while/body/eval_jaxpr/ppermute | solution.py:14
  156.7 2.6 convolution_add_fusion.4
  159.3 5.4 %collective-permute-start = (f32[8,2,128]{2,1,0:T(2,128)}, f32[8,2,128]{2,1,0:T(2,128)S(1)}, u32[]{:S(2)}, u32[]{:S(2)}) collective-permute-start(f32[8,2,128]{2,1,0:T(2,128)} %convolution_add_fusion.4), channel_id=1, source_target_pairs={{0,1},{1,2},{2,3},{3,4},{4,5},{5,6},{6,7},{7,8},{8,9},{9,10},{10,1... | collective-permute-start | bytes 24584 | tf_op jit(solution)/shard_map/while/body/eval_jaxpr/ppermute | solution.py:14
  165.7 2.6 convolution_add_fusion.4
  168.2 5.4 %collective-permute-start = (f32[8,2,128]{2,1,0:T(2,128)}, f32[8,2,128]{2,1,0:T(2,128)S(1)}, u32[]{:S(2)}, u32[]{:S(2)}) collective-permute-start(f32[8,2,128]{2,1,0:T(2,128)} %convolution_add_fusion.4), channel_id=1, source_target_pairs={{0,1},{1,2},{2,3},{3,4},{4,5},{5,6},{6,7},{7,8},{8,9},{9,10},{10,1... | collective-permute-start | bytes 24584 | tf_op jit(solution)/shard_map/while/body/eval_jaxpr/ppermute | solution.py:14
  174.6 2.6 convolution_add_fusion.4
  177.2 5.4 %collective-permute-start = (f32[8,2,128]{2,1,0:T(2,128)}, f32[8,2,128]{2,1,0:T(2,128)S(1)}, u32[]{:S(2)}, u32[]{:S(2)}) collective-permute-start(f32[8,2,128]{2,1,0:T(2,128)} %convolution_add_fusion.4), channel_id=1, source_target_pairs={{0,1},{1,2},{2,3},{3,4},{4,5},{5,6},{6,7},{7,8},{8,9},{9,10},{10,1... | collective-permute-start | bytes 24584 | tf_op jit(solution)/shard_map/while/body/eval_jaxpr/ppermute | solution.py:14
  183.6 2.6 convolution_add_fusion.4
  186.1 5.4 %collective-permute-start = (f32[8,2,128]{2,1,0:T(2,128)}, f32[8,2,128]{2,1,0:T(2,128)S(1)}, u32[]{:S(2)}, u32[]{:S(2)}) collective-permute-start(f32[8,2,128]{2,1,0:T(2,128)} %convolution_add_fusion.4), channel_id=1, source_target_pairs={{0,1},{1,2},{2,3},{3,4},{4,5},{5,6},{6,7},{7,8},{8,9},{9,10},{10,1... | collective-permute-start | bytes 24584 | tf_op jit(solution)/shard_map/while/body/eval_jaxpr/ppermute | solution.py:14
  203.3 134.7 %while.21 = (s32[]{:T(128)}, f32[8,2,128]{2,1,0:T(2,128)S(1)}, f32[8,128,128]{2,1,0:T(8,128)}, f32[8,2,128]{2,1,0:T(2,128)S(1)}, s32[]{:T(128)}) while((s32[]{:T(128)}, f32[8,2,128]{2,1,0:T(2,128)S(1)}, f32[8,128,128]{2,1,0:T(8,128)}, f32[8,2,128]{2,1,0:T(2,128)S(1)}, s32[]{:T(128)}) %tuple.40), condition=%wide.region_3.4_spmd, body=%wide.region_2.3_spmd.sunk | while | flops 3147778 | bytes 581733 | solution.py:132
  203.3 2.6 convolution_add_fusion.5
  207.8 5.0 %collective-permute-done.1 = f32[8,2,128]{2,1,0:T(2,128)S(1)} collective-permute-done((f32[8,2,128]{2,1,0:T(2,128)}, f32[8,2,128]{2,1,0:T(2,128)S(1)}, u32[]{:S(2)}, u32[]{:S(2)}) %collective-permute-start.1) | collective-permute-done | bytes 8224 | tf_op jit(solution)/shard_map/while/body/eval_jaxpr/ppermute | solution.py:14
  212.8 2.6 convolution_add_fusion.5
  217.3 4.5 %collective-permute-done.1 = f32[8,2,128]{2,1,0:T(2,128)S(1)} collective-permute-done((f32[8,2,128]{2,1,0:T(2,128)}, f32[8,2,128]{2,1,0:T(2,128)S(1)}, u32[]{:S(2)}, u32[]{:S(2)}) %collective-permute-start.1) | collective-permute-done | bytes 8224 | tf_op jit(solution)/shard_map/while/body/eval_jaxpr/ppermute | solution.py:14
  221.7 2.6 convolution_add_fusion.5
  226.2 4.5 %collective-permute-done.1 = f32[8,2,128]{2,1,0:T(2,128)S(1)} collective-permute-done((f32[8,2,128]{2,1,0:T(2,128)}, f32[8,2,128]{2,1,0:T(2,128)S(1)}, u32[]{:S(2)}, u32[]{:S(2)}) %collective-permute-start.1) | collective-permute-done | bytes 8224 | tf_op jit(solution)/shard_map/while/body/eval_jaxpr/ppermute | solution.py:14
  230.7 2.6 convolution_add_fusion.5
  235.2 4.5 %collective-permute-done.1 = f32[8,2,128]{2,1,0:T(2,128)S(1)} collective-permute-done((f32[8,2,128]{2,1,0:T(2,128)}, f32[8,2,128]{2,1,0:T(2,128)S(1)}, u32[]{:S(2)}, u32[]{:S(2)}) %collective-permute-start.1) | collective-permute-done | bytes 8224 | tf_op jit(solution)/shard_map/while/body/eval_jaxpr/ppermute | solution.py:14
  239.6 2.6 convolution_add_fusion.5
  244.1 4.5 %collective-permute-done.1 = f32[8,2,128]{2,1,0:T(2,128)S(1)} collective-permute-done((f32[8,2,128]{2,1,0:T(2,128)}, f32[8,2,128]{2,1,0:T(2,128)S(1)}, u32[]{:S(2)}, u32[]{:S(2)}) %collective-permute-start.1) | collective-permute-done | bytes 8224 | tf_op jit(solution)/shard_map/while/body/eval_jaxpr/ppermute | solution.py:14
  248.6 2.6 convolution_add_fusion.5
  253.0 4.5 %collective-permute-done.1 = f32[8,2,128]{2,1,0:T(2,128)S(1)} collective-permute-done((f32[8,2,128]{2,1,0:T(2,128)}, f32[8,2,128]{2,1,0:T(2,128)S(1)}, u32[]{:S(2)}, u32[]{:S(2)}) %collective-permute-start.1) | collective-permute-done | bytes 8224 | tf_op jit(solution)/shard_map/while/body/eval_jaxpr/ppermute | solution.py:14
  257.5 2.6 convolution_add_fusion.5
  262.0 4.5 %collective-permute-done.1 = f32[8,2,128]{2,1,0:T(2,128)S(1)} collective-permute-done((f32[8,2,128]{2,1,0:T(2,128)}, f32[8,2,128]{2,1,0:T(2,128)S(1)}, u32[]{:S(2)}, u32[]{:S(2)}) %collective-permute-start.1) | collective-permute-done | bytes 8224 | tf_op jit(solution)/shard_map/while/body/eval_jaxpr/ppermute | solution.py:14
  266.4 2.6 convolution_add_fusion.5
  270.9 4.5 %collective-permute-done.1 = f32[8,2,128]{2,1,0:T(2,128)S(1)} collective-permute-done((f32[8,2,128]{2,1,0:T(2,128)}, f32[8,2,128]{2,1,0:T(2,128)S(1)}, u32[]{:S(2)}, u32[]{:S(2)}) %collective-permute-start.1) | collective-permute-done | bytes 8224 | tf_op jit(solution)/shard_map/while/body/eval_jaxpr/ppermute | solution.py:14
  275.4 2.6 convolution_add_fusion.5
  279.9 4.5 %collective-permute-done.1 = f32[8,2,128]{2,1,0:T(2,128)S(1)} collective-permute-done((f32[8,2,128]{2,1,0:T(2,128)}, f32[8,2,128]{2,1,0:T(2,128)S(1)}, u32[]{:S(2)}, u32[]{:S(2)}) %collective-permute-start.1) | collective-permute-done | bytes 8224 | tf_op jit(solution)/shard_map/while/body/eval_jaxpr/ppermute | solution.py:14
  284.3 2.6 convolution_add_fusion.5
  288.8 4.5 %collective-permute-done.1 = f32[8,2,128]{2,1,0:T(2,128)S(1)} collective-permute-done((f32[8,2,128]{2,1,0:T(2,128)}, f32[8,2,128]{2,1,0:T(2,128)S(1)}, u32[]{:S(2)}, u32[]{:S(2)}) %collective-permute-start.1) | collective-permute-done | bytes 8224 | tf_op jit(solution)/shard_map/while/body/eval_jaxpr/ppermute | solution.py:14
  293.3 2.6 convolution_add_fusion.5
  297.8 4.5 %collective-permute-done.1 = f32[8,2,128]{2,1,0:T(2,128)S(1)} collective-permute-done((f32[8,2,128]{2,1,0:T(2,128)}, f32[8,2,128]{2,1,0:T(2,128)S(1)}, u32[]{:S(2)}, u32[]{:S(2)}) %collective-permute-start.1) | collective-permute-done | bytes 8224 | tf_op jit(solution)/shard_map/while/body/eval_jaxpr/ppermute | solution.py:14
  302.2 2.6 convolution_add_fusion.5
  306.7 4.5 %collective-permute-done.1 = f32[8,2,128]{2,1,0:T(2,128)S(1)} collective-permute-done((f32[8,2,128]{2,1,0:T(2,128)}, f32[8,2,128]{2,1,0:T(2,128)S(1)}, u32[]{:S(2)}, u32[]{:S(2)}) %collective-permute-start.1) | collective-permute-done | bytes 8224 | tf_op jit(solution)/shard_map/while/body/eval_jaxpr/ppermute | solution.py:14
  311.2 2.6 convolution_add_fusion.5
  315.6 4.5 %collective-permute-done.1 = f32[8,2,128]{2,1,0:T(2,128)S(1)} collective-permute-done((f32[8,2,128]{2,1,0:T(2,128)}, f32[8,2,128]{2,1,0:T(2,128)S(1)}, u32[]{:S(2)}, u32[]{:S(2)}) %collective-permute-start.1) | collective-permute-done | bytes 8224 | tf_op jit(solution)/shard_map/while/body/eval_jaxpr/ppermute | solution.py:14
  320.1 2.6 convolution_add_fusion.5
  324.6 4.5 %collective-permute-done.1 = f32[8,2,128]{2,1,0:T(2,128)S(1)} collective-permute-done((f32[8,2,128]{2,1,0:T(2,128)}, f32[8,2,128]{2,1,0:T(2,128)S(1)}, u32[]{:S(2)}, u32[]{:S(2)}) %collective-permute-start.1) | collective-permute-done | bytes 8224 | tf_op jit(solution)/shard_map/while/body/eval_jaxpr/ppermute | solution.py:14
  333.5 4.5 %collective-permute-done.1 = f32[8,2,128]{2,1,0:T(2,128)S(1)} collective-permute-done((f32[8,2,128]{2,1,0:T(2,128)}, f32[8,2,128]{2,1,0:T(2,128)S(1)}, u32[]{:S(2)}, u32[]{:S(2)}) %collective-permute-start.1) | collective-permute-done | bytes 8224 | tf_op jit(solution)/shard_map/while/body/eval_jaxpr/ppermute | solution.py:14
  (171 shorter events, 107.8 us)
Async XLA Ops:
  0.0 45.3 %copy-start = (f32[3,128,128]{2,1,0:T(8,128)S(1)}, f32[3,128,128]{2,1,0:T(8,128)}, u32[]{:S(2)}) copy-start(f32[3,128,128]{2,1,0:T(8,128)} %param.16) | copy-start | bytes 589828
  0.0 18.0 %copy-start.8 = (f32[2,3,128,128]{3,2,1,0:T(8,128)S(1)}, f32[2,3,128,128]{3,2,1,0:T(8,128)}, u32[]{:S(2)}) copy-start(f32[2,3,128,128]{3,2,1,0:T(8,128)} %param.24) | copy-start | bytes 1179652
  7.4 35.0 %all-to-all-start = ((f32[32,16,96]{2,1,0:T(8,128)}), f32[32,16,96]{2,1,0:T(8,128)}, u32[]{:S(2)}, u32[]{:S(2)}) async-start(f32[32,16,96]{2,1,0:T(8,128)} %bitcast), calls=%async_computation | async-start | bytes 524288 | tf_op jit(solution)/shard_map/all_to_all | solution.py:58
  18.7 21.1 %copy-start.21 = (f32[8]{0:T(128)}, f32[8]{0:T(128)S(1)}, u32[]{:S(2)}) copy-start(f32[8]{0:T(128)S(1)} %multiply_multiply_fusion) | copy-start | bytes 100
  18.7 4.9 %copy-start.1 = (f32[8,3,128,128]{3,2,1,0:T(8,128)S(1)}, f32[8,3,128,128]{3,2,1,0:T(8,128)}, u32[]{:S(2)}) copy-start(f32[8,3,128,128]{3,2,1,0:T(8,128)} %param.25) | copy-start | bytes 4718596
  18.7 4.9 %copy-start.7 = (f32[128,128]{0,1:T(8,128)S(1)}, f32[128,128]{0,1:T(8,128)}, u32[]{:S(2)}) copy-start(f32[128,128]{0,1:T(8,128)} %fusion.110) | copy-start | bytes 196612
  37.6 2.1 copy-start.24
  37.7 2.1 copy-start.25
  40.6 5.1 %copy-start.16 = (f32[3,7,7]{2,1,0:T(8,128)S(1)}, f32[3,7,7]{2,1,0:T(8,128)}, u32[]{:S(2)}) copy-start(f32[3,7,7]{2,1,0:T(8,128)} %param.17) | copy-start | bytes 1768
  42.4 5.6 %copy-start.19 = (f32[3,2,7]{2,1,0:T(2,128)S(1)}, f32[3,2,7]{2,1,0:T(2,128)}, u32[]{:S(2)}) copy-start(f32[3,2,7]{2,1,0:T(2,128)} %param.22) | copy-start | bytes 508
  45.3 1.9 copy-start.2
  45.3 3.1 copy-start.3
  45.3 3.3 copy-start.5
  45.3 3.3 copy-start.22
  45.3 3.6 %copy-start.26 = (s32[3,2,128]{2,1,0:T(2,128)S(1)}, s32[3,2,128]{2,1,0:T(2,128)}, u32[]{:S(2)}) copy-start(s32[3,2,128]{2,1,0:T(2,128)} %param.23) | copy-start | bytes 9220
  45.7 11.3 %copy-start.18 = (f32[8,2,128]{2,1,0:T(2,128)S(1)}, f32[8,2,128]{2,1,0:T(2,128)}, u32[]{:S(2)}) copy-start(f32[8,2,128]{2,1,0:T(2,128)} %fusion.62) | copy-start | bytes 24580
  49.3 7.7 %collective-permute-start.2 = (f32[8,2,128]{2,0,1:T(8,128)S(1)}, f32[8,2,128]{2,0,1:T(8,128)S(1)}, u32[]{:S(2)}, u32[]{:S(2)}) collective-permute-start(f32[8,2,128]{2,0,1:T(8,128)S(1)} %slice_bitcast_fusion.27), channel_id=1, source_target_pairs={{1,0},{2,1},{3,2},{4,3},{5,4},{6,5},{7,6},{8,7},{9,8},{10,9},{11,1... | collective-permute-start | bytes 24584 | tf_op jit(solution)/shard_map/ppermute | solution.py:14
  57.0 3.8 %copy-start.9 = (f32[8,2,3,128]{3,0,1,2:T(8,128)}, f32[8,2,3,128]{3,0,1,2:T(8,128)S(1)}, u32[]{:S(2)}) copy-start(f32[8,2,3,128]{3,0,1,2:T(8,128)S(1)} %fusion.117) | copy-start | bytes 73732
  64.3 3.3 collective-permute-start
  70.2 6.0 %collective-permute-start = (f32[8,2,128]{2,1,0:T(2,128)}, f32[8,2,128]{2,1,0:T(2,128)S(1)}, u32[]{:S(2)}, u32[]{:S(2)}) collective-permute-start(f32[8,2,128]{2,1,0:T(2,128)} %convolution_add_fusion.4), channel_id=1, source_target_pairs={{0,1},{1,2},{2,3},{3,4},{4,5},{5,6},{6,7},{7,8},{8,9},{9,10},{10,1... | collective-permute-start | bytes 24584 | tf_op jit(solution)/shard_map/while/body/eval_jaxpr/ppermute | solution.py:14
  78.8 6.4 %collective-permute-start = (f32[8,2,128]{2,1,0:T(2,128)}, f32[8,2,128]{2,1,0:T(2,128)S(1)}, u32[]{:S(2)}, u32[]{:S(2)}) collective-permute-start(f32[8,2,128]{2,1,0:T(2,128)} %convolution_add_fusion.4), channel_id=1, source_target_pairs={{0,1},{1,2},{2,3},{3,4},{4,5},{5,6},{6,7},{7,8},{8,9},{9,10},{10,1... | collective-permute-start | bytes 24584 | tf_op jit(solution)/shard_map/while/body/eval_jaxpr/ppermute | solution.py:14
  87.7 6.4 %collective-permute-start = (f32[8,2,128]{2,1,0:T(2,128)}, f32[8,2,128]{2,1,0:T(2,128)S(1)}, u32[]{:S(2)}, u32[]{:S(2)}) collective-permute-start(f32[8,2,128]{2,1,0:T(2,128)} %convolution_add_fusion.4), channel_id=1, source_target_pairs={{0,1},{1,2},{2,3},{3,4},{4,5},{5,6},{6,7},{7,8},{8,9},{9,10},{10,1... | collective-permute-start | bytes 24584 | tf_op jit(solution)/shard_map/while/body/eval_jaxpr/ppermute | solution.py:14
  96.7 6.4 %collective-permute-start = (f32[8,2,128]{2,1,0:T(2,128)}, f32[8,2,128]{2,1,0:T(2,128)S(1)}, u32[]{:S(2)}, u32[]{:S(2)}) collective-permute-start(f32[8,2,128]{2,1,0:T(2,128)} %convolution_add_fusion.4), channel_id=1, source_target_pairs={{0,1},{1,2},{2,3},{3,4},{4,5},{5,6},{6,7},{7,8},{8,9},{9,10},{10,1... | collective-permute-start | bytes 24584 | tf_op jit(solution)/shard_map/while/body/eval_jaxpr/ppermute | solution.py:14
  105.6 6.4 %collective-permute-start = (f32[8,2,128]{2,1,0:T(2,128)}, f32[8,2,128]{2,1,0:T(2,128)S(1)}, u32[]{:S(2)}, u32[]{:S(2)}) collective-permute-start(f32[8,2,128]{2,1,0:T(2,128)} %convolution_add_fusion.4), channel_id=1, source_target_pairs={{0,1},{1,2},{2,3},{3,4},{4,5},{5,6},{6,7},{7,8},{8,9},{9,10},{10,1... | collective-permute-start | bytes 24584 | tf_op jit(solution)/shard_map/while/body/eval_jaxpr/ppermute | solution.py:14
  114.5 6.4 %collective-permute-start = (f32[8,2,128]{2,1,0:T(2,128)}, f32[8,2,128]{2,1,0:T(2,128)S(1)}, u32[]{:S(2)}, u32[]{:S(2)}) collective-permute-start(f32[8,2,128]{2,1,0:T(2,128)} %convolution_add_fusion.4), channel_id=1, source_target_pairs={{0,1},{1,2},{2,3},{3,4},{4,5},{5,6},{6,7},{7,8},{8,9},{9,10},{10,1... | collective-permute-start | bytes 24584 | tf_op jit(solution)/shard_map/while/body/eval_jaxpr/ppermute | solution.py:14
  123.5 6.4 %collective-permute-start = (f32[8,2,128]{2,1,0:T(2,128)}, f32[8,2,128]{2,1,0:T(2,128)S(1)}, u32[]{:S(2)}, u32[]{:S(2)}) collective-permute-start(f32[8,2,128]{2,1,0:T(2,128)} %convolution_add_fusion.4), channel_id=1, source_target_pairs={{0,1},{1,2},{2,3},{3,4},{4,5},{5,6},{6,7},{7,8},{8,9},{9,10},{10,1... | collective-permute-start | bytes 24584 | tf_op jit(solution)/shard_map/while/body/eval_jaxpr/ppermute | solution.py:14
  132.4 6.4 %collective-permute-start = (f32[8,2,128]{2,1,0:T(2,128)}, f32[8,2,128]{2,1,0:T(2,128)S(1)}, u32[]{:S(2)}, u32[]{:S(2)}) collective-permute-start(f32[8,2,128]{2,1,0:T(2,128)} %convolution_add_fusion.4), channel_id=1, source_target_pairs={{0,1},{1,2},{2,3},{3,4},{4,5},{5,6},{6,7},{7,8},{8,9},{9,10},{10,1... | collective-permute-start | bytes 24584 | tf_op jit(solution)/shard_map/while/body/eval_jaxpr/ppermute | solution.py:14
  141.4 6.4 %collective-permute-start = (f32[8,2,128]{2,1,0:T(2,128)}, f32[8,2,128]{2,1,0:T(2,128)S(1)}, u32[]{:S(2)}, u32[]{:S(2)}) collective-permute-start(f32[8,2,128]{2,1,0:T(2,128)} %convolution_add_fusion.4), channel_id=1, source_target_pairs={{0,1},{1,2},{2,3},{3,4},{4,5},{5,6},{6,7},{7,8},{8,9},{9,10},{10,1... | collective-permute-start | bytes 24584 | tf_op jit(solution)/shard_map/while/body/eval_jaxpr/ppermute | solution.py:14
  150.3 6.4 %collective-permute-start = (f32[8,2,128]{2,1,0:T(2,128)}, f32[8,2,128]{2,1,0:T(2,128)S(1)}, u32[]{:S(2)}, u32[]{:S(2)}) collective-permute-start(f32[8,2,128]{2,1,0:T(2,128)} %convolution_add_fusion.4), channel_id=1, source_target_pairs={{0,1},{1,2},{2,3},{3,4},{4,5},{5,6},{6,7},{7,8},{8,9},{9,10},{10,1... | collective-permute-start | bytes 24584 | tf_op jit(solution)/shard_map/while/body/eval_jaxpr/ppermute | solution.py:14
  159.3 6.4 %collective-permute-start = (f32[8,2,128]{2,1,0:T(2,128)}, f32[8,2,128]{2,1,0:T(2,128)S(1)}, u32[]{:S(2)}, u32[]{:S(2)}) collective-permute-start(f32[8,2,128]{2,1,0:T(2,128)} %convolution_add_fusion.4), channel_id=1, source_target_pairs={{0,1},{1,2},{2,3},{3,4},{4,5},{5,6},{6,7},{7,8},{8,9},{9,10},{10,1... | collective-permute-start | bytes 24584 | tf_op jit(solution)/shard_map/while/body/eval_jaxpr/ppermute | solution.py:14
  168.2 6.4 %collective-permute-start = (f32[8,2,128]{2,1,0:T(2,128)}, f32[8,2,128]{2,1,0:T(2,128)S(1)}, u32[]{:S(2)}, u32[]{:S(2)}) collective-permute-start(f32[8,2,128]{2,1,0:T(2,128)} %convolution_add_fusion.4), channel_id=1, source_target_pairs={{0,1},{1,2},{2,3},{3,4},{4,5},{5,6},{6,7},{7,8},{8,9},{9,10},{10,1... | collective-permute-start | bytes 24584 | tf_op jit(solution)/shard_map/while/body/eval_jaxpr/ppermute | solution.py:14
  177.2 6.4 %collective-permute-start = (f32[8,2,128]{2,1,0:T(2,128)}, f32[8,2,128]{2,1,0:T(2,128)S(1)}, u32[]{:S(2)}, u32[]{:S(2)}) collective-permute-start(f32[8,2,128]{2,1,0:T(2,128)} %convolution_add_fusion.4), channel_id=1, source_target_pairs={{0,1},{1,2},{2,3},{3,4},{4,5},{5,6},{6,7},{7,8},{8,9},{9,10},{10,1... | collective-permute-start | bytes 24584 | tf_op jit(solution)/shard_map/while/body/eval_jaxpr/ppermute | solution.py:14
  186.1 6.4 %collective-permute-start = (f32[8,2,128]{2,1,0:T(2,128)}, f32[8,2,128]{2,1,0:T(2,128)S(1)}, u32[]{:S(2)}, u32[]{:S(2)}) collective-permute-start(f32[8,2,128]{2,1,0:T(2,128)} %convolution_add_fusion.4), channel_id=1, source_target_pairs={{0,1},{1,2},{2,3},{3,4},{4,5},{5,6},{6,7},{7,8},{8,9},{9,10},{10,1... | collective-permute-start | bytes 24584 | tf_op jit(solution)/shard_map/while/body/eval_jaxpr/ppermute | solution.py:14
  192.5 3.5 %copy-start.10 = (f32[8,2,3,128]{3,0,1,2:T(8,128)S(1)}, f32[8,2,3,128]{3,0,1,2:T(8,128)}, u32[]{:S(2)}) copy-start(f32[8,2,3,128]{3,0,1,2:T(8,128)} %copy-done.9) | copy-start | bytes 73732
  195.1 6.7 %copy-start.11 = (f32[8,2,128]{2,1,0:T(2,128)}, f32[8,2,128]{2,1,0:T(2,128)S(1)}, u32[]{:S(2)}) copy-start(f32[8,2,128]{2,1,0:T(2,128)S(1)} %fusion.44) | copy-start | bytes 24580
  196.9 4.8 %copy-start.13 = (f32[8,2,128]{2,1,0:T(2,128)}, f32[8,2,128]{2,1,0:T(2,128)S(1)}, u32[]{:S(2)}) copy-start(f32[8,2,128]{2,1,0:T(2,128)S(1)} %fusion.35) | copy-start | bytes 24580
  198.8 4.4 %copy-start.15 = (f32[8,2,128]{2,1,0:T(2,128)}, f32[8,2,128]{2,1,0:T(2,128)S(1)}, u32[]{:S(2)}) copy-start(f32[8,2,128]{2,1,0:T(2,128)S(1)} %fusion.26) | copy-start | bytes 24580
  205.9 6.9 %collective-permute-start.1 = (f32[8,2,128]{2,1,0:T(2,128)}, f32[8,2,128]{2,1,0:T(2,128)S(1)}, u32[]{:S(2)}, u32[]{:S(2)}) collective-permute-start(f32[8,2,128]{2,1,0:T(2,128)} %convolution_add_fusion.5), channel_id=1, source_target_pairs={{1,0},{2,1},{3,2},{4,3},{5,4},{6,5},{7,6},{8,7},{9,8},{10,9},{11,1... | collective-permute-start | bytes 24584 | tf_op jit(solution)/shard_map/while/body/eval_jaxpr/ppermute | solution.py:14
  215.3 6.4 %collective-permute-start.1 = (f32[8,2,128]{2,1,0:T(2,128)}, f32[8,2,128]{2,1,0:T(2,128)S(1)}, u32[]{:S(2)}, u32[]{:S(2)}) collective-permute-start(f32[8,2,128]{2,1,0:T(2,128)} %convolution_add_fusion.5), channel_id=1, source_target_pairs={{1,0},{2,1},{3,2},{4,3},{5,4},{6,5},{7,6},{8,7},{9,8},{10,9},{11,1... | collective-permute-start | bytes 24584 | tf_op jit(solution)/shard_map/while/body/eval_jaxpr/ppermute | solution.py:14
  224.3 6.4 %collective-permute-start.1 = (f32[8,2,128]{2,1,0:T(2,128)}, f32[8,2,128]{2,1,0:T(2,128)S(1)}, u32[]{:S(2)}, u32[]{:S(2)}) collective-permute-start(f32[8,2,128]{2,1,0:T(2,128)} %convolution_add_fusion.5), channel_id=1, source_target_pairs={{1,0},{2,1},{3,2},{4,3},{5,4},{6,5},{7,6},{8,7},{9,8},{10,9},{11,1... | collective-permute-start | bytes 24584 | tf_op jit(solution)/shard_map/while/body/eval_jaxpr/ppermute | solution.py:14
  233.2 6.4 %collective-permute-start.1 = (f32[8,2,128]{2,1,0:T(2,128)}, f32[8,2,128]{2,1,0:T(2,128)S(1)}, u32[]{:S(2)}, u32[]{:S(2)}) collective-permute-start(f32[8,2,128]{2,1,0:T(2,128)} %convolution_add_fusion.5), channel_id=1, source_target_pairs={{1,0},{2,1},{3,2},{4,3},{5,4},{6,5},{7,6},{8,7},{9,8},{10,9},{11,1... | collective-permute-start | bytes 24584 | tf_op jit(solution)/shard_map/while/body/eval_jaxpr/ppermute | solution.py:14
  242.2 6.4 %collective-permute-start.1 = (f32[8,2,128]{2,1,0:T(2,128)}, f32[8,2,128]{2,1,0:T(2,128)S(1)}, u32[]{:S(2)}, u32[]{:S(2)}) collective-permute-start(f32[8,2,128]{2,1,0:T(2,128)} %convolution_add_fusion.5), channel_id=1, source_target_pairs={{1,0},{2,1},{3,2},{4,3},{5,4},{6,5},{7,6},{8,7},{9,8},{10,9},{11,1... | collective-permute-start | bytes 24584 | tf_op jit(solution)/shard_map/while/body/eval_jaxpr/ppermute | solution.py:14
  251.1 6.4 %collective-permute-start.1 = (f32[8,2,128]{2,1,0:T(2,128)}, f32[8,2,128]{2,1,0:T(2,128)S(1)}, u32[]{:S(2)}, u32[]{:S(2)}) collective-permute-start(f32[8,2,128]{2,1,0:T(2,128)} %convolution_add_fusion.5), channel_id=1, source_target_pairs={{1,0},{2,1},{3,2},{4,3},{5,4},{6,5},{7,6},{8,7},{9,8},{10,9},{11,1... | collective-permute-start | bytes 24584 | tf_op jit(solution)/shard_map/while/body/eval_jaxpr/ppermute | solution.py:14
  260.1 6.4 %collective-permute-start.1 = (f32[8,2,128]{2,1,0:T(2,128)}, f32[8,2,128]{2,1,0:T(2,128)S(1)}, u32[]{:S(2)}, u32[]{:S(2)}) collective-permute-start(f32[8,2,128]{2,1,0:T(2,128)} %convolution_add_fusion.5), channel_id=1, source_target_pairs={{1,0},{2,1},{3,2},{4,3},{5,4},{6,5},{7,6},{8,7},{9,8},{10,9},{11,1... | collective-permute-start | bytes 24584 | tf_op jit(solution)/shard_map/while/body/eval_jaxpr/ppermute | solution.py:14
  269.0 6.4 %collective-permute-start.1 = (f32[8,2,128]{2,1,0:T(2,128)}, f32[8,2,128]{2,1,0:T(2,128)S(1)}, u32[]{:S(2)}, u32[]{:S(2)}) collective-permute-start(f32[8,2,128]{2,1,0:T(2,128)} %convolution_add_fusion.5), channel_id=1, source_target_pairs={{1,0},{2,1},{3,2},{4,3},{5,4},{6,5},{7,6},{8,7},{9,8},{10,9},{11,1... | collective-permute-start | bytes 24584 | tf_op jit(solution)/shard_map/while/body/eval_jaxpr/ppermute | solution.py:14
  277.9 6.4 %collective-permute-start.1 = (f32[8,2,128]{2,1,0:T(2,128)}, f32[8,2,128]{2,1,0:T(2,128)S(1)}, u32[]{:S(2)}, u32[]{:S(2)}) collective-permute-start(f32[8,2,128]{2,1,0:T(2,128)} %convolution_add_fusion.5), channel_id=1, source_target_pairs={{1,0},{2,1},{3,2},{4,3},{5,4},{6,5},{7,6},{8,7},{9,8},{10,9},{11,1... | collective-permute-start | bytes 24584 | tf_op jit(solution)/shard_map/while/body/eval_jaxpr/ppermute | solution.py:14
  286.9 6.4 %collective-permute-start.1 = (f32[8,2,128]{2,1,0:T(2,128)}, f32[8,2,128]{2,1,0:T(2,128)S(1)}, u32[]{:S(2)}, u32[]{:S(2)}) collective-permute-start(f32[8,2,128]{2,1,0:T(2,128)} %convolution_add_fusion.5), channel_id=1, source_target_pairs={{1,0},{2,1},{3,2},{4,3},{5,4},{6,5},{7,6},{8,7},{9,8},{10,9},{11,1... | collective-permute-start | bytes 24584 | tf_op jit(solution)/shard_map/while/body/eval_jaxpr/ppermute | solution.py:14
  295.8 6.4 %collective-permute-start.1 = (f32[8,2,128]{2,1,0:T(2,128)}, f32[8,2,128]{2,1,0:T(2,128)S(1)}, u32[]{:S(2)}, u32[]{:S(2)}) collective-permute-start(f32[8,2,128]{2,1,0:T(2,128)} %convolution_add_fusion.5), channel_id=1, source_target_pairs={{1,0},{2,1},{3,2},{4,3},{5,4},{6,5},{7,6},{8,7},{9,8},{10,9},{11,1... | collective-permute-start | bytes 24584 | tf_op jit(solution)/shard_map/while/body/eval_jaxpr/ppermute | solution.py:14
  304.8 6.4 %collective-permute-start.1 = (f32[8,2,128]{2,1,0:T(2,128)}, f32[8,2,128]{2,1,0:T(2,128)S(1)}, u32[]{:S(2)}, u32[]{:S(2)}) collective-permute-start(f32[8,2,128]{2,1,0:T(2,128)} %convolution_add_fusion.5), channel_id=1, source_target_pairs={{1,0},{2,1},{3,2},{4,3},{5,4},{6,5},{7,6},{8,7},{9,8},{10,9},{11,1... | collective-permute-start | bytes 24584 | tf_op jit(solution)/shard_map/while/body/eval_jaxpr/ppermute | solution.py:14
  313.7 6.4 %collective-permute-start.1 = (f32[8,2,128]{2,1,0:T(2,128)}, f32[8,2,128]{2,1,0:T(2,128)S(1)}, u32[]{:S(2)}, u32[]{:S(2)}) collective-permute-start(f32[8,2,128]{2,1,0:T(2,128)} %convolution_add_fusion.5), channel_id=1, source_target_pairs={{1,0},{2,1},{3,2},{4,3},{5,4},{6,5},{7,6},{8,7},{9,8},{10,9},{11,1... | collective-permute-start | bytes 24584 | tf_op jit(solution)/shard_map/while/body/eval_jaxpr/ppermute | solution.py:14
  322.7 6.4 %collective-permute-start.1 = (f32[8,2,128]{2,1,0:T(2,128)}, f32[8,2,128]{2,1,0:T(2,128)S(1)}, u32[]{:S(2)}, u32[]{:S(2)}) collective-permute-start(f32[8,2,128]{2,1,0:T(2,128)} %convolution_add_fusion.5), channel_id=1, source_target_pairs={{1,0},{2,1},{3,2},{4,3},{5,4},{6,5},{7,6},{8,7},{9,8},{10,9},{11,1... | collective-permute-start | bytes 24584 | tf_op jit(solution)/shard_map/while/body/eval_jaxpr/ppermute | solution.py:14
  331.6 6.4 %collective-permute-start.1 = (f32[8,2,128]{2,1,0:T(2,128)}, f32[8,2,128]{2,1,0:T(2,128)S(1)}, u32[]{:S(2)}, u32[]{:S(2)}) collective-permute-start(f32[8,2,128]{2,1,0:T(2,128)} %convolution_add_fusion.5), channel_id=1, source_target_pairs={{1,0},{2,1},{3,2},{4,3},{5,4},{6,5},{7,6},{8,7},{9,8},{10,9},{11,1... | collective-permute-start | bytes 24584 | tf_op jit(solution)/shard_map/while/body/eval_jaxpr/ppermute | solution.py:14
  338.0 6.6 %copy-start.12 = (f32[8,2,128]{2,1,0:T(2,128)S(1)}, f32[8,2,128]{2,1,0:T(2,128)}, u32[]{:S(2)}) copy-start(f32[8,2,128]{2,1,0:T(2,128)} %copy-done.11) | copy-start | bytes 24580
  338.0 7.6 %copy-start.27 = (s32[3,2,128]{2,1,0:T(2,128)S(1)}, s32[3,2,128]{2,1,0:T(2,128)}, u32[]{:S(2)}) copy-start(s32[3,2,128]{2,1,0:T(2,128)} %param.23) | copy-start | bytes 9220
  338.0 8.1 %copy-start.4 = (f32[3,128,128]{2,1,0:T(8,128)S(1)}, f32[3,128,128]{2,1,0:T(8,128)}, u32[]{:S(2)}) copy-start(f32[3,128,128]{2,1,0:T(8,128)} %param.20) | copy-start | bytes 589828
  339.6 6.9 %copy-start.6 = (f32[3,128,128]{2,1,0:T(8,128)S(1)}, f32[3,128,128]{2,1,0:T(8,128)}, u32[]{:S(2)}) copy-start(f32[3,128,128]{2,1,0:T(8,128)} %param.21) | copy-start | bytes 589828
  339.7 6.9 %copy-start.23 = (f32[8]{0:T(128)S(1)}, f32[8]{0:T(128)}, u32[]{:S(2)}) copy-start(f32[8]{0:T(128)} %copy-done.21) | copy-start | bytes 100
  339.7 7.3 %copy-start.20 = (f32[3,2,7]{2,1,0:T(2,128)S(1)}, f32[3,2,7]{2,1,0:T(2,128)}, u32[]{:S(2)}) copy-start(f32[3,2,7]{2,1,0:T(2,128)} %param.22) | copy-start | bytes 508
  340.2 5.3 %collective-permute-start.3 = (f32[8,2,128]{2,1,0:T(2,128)S(1)}, f32[8,2,128]{2,1,0:T(2,128)S(1)}, u32[]{:S(2)}, u32[]{:S(2)}) collective-permute-start(f32[8,2,128]{2,1,0:T(2,128)S(1)} %convolution_subtract_fusion.2), channel_id=1, source_target_pairs={{0,1},{1,2},{2,3},{3,4},{4,5},{5,6},{6,7},{7,8},{8,9},{9,10},{10,1... | collective-permute-start | bytes 24584 | tf_op jit(solution)/shard_map/ppermute | solution.py:14
  344.0 3.7 %copy-start.14 = (f32[8,3,7,128]{3,2,0,1:T(8,128)S(1)}, f32[8,3,7,128]{3,2,0,1:T(8,128)}, u32[]{:S(2)}) copy-start(f32[8,3,7,128]{3,2,0,1:T(8,128)} %broadcast_add_fusion) | copy-start | bytes 258052
  344.0 3.7 %copy-start.17 = (f32[3,7,7]{2,1,0:T(8,128)S(1)}, f32[3,7,7]{2,1,0:T(8,128)}, u32[]{:S(2)}) copy-start(f32[3,7,7]{2,1,0:T(8,128)} %param.17) | copy-start | bytes 1768
where the time goes:
time: 353 us; the launch traced here: 350 us
  matrix products  131 us (37%)
  starting transfers between devices  121 us (34%)
  waiting for transfers between devices  86 us (24%)
  local copies, waits for them, and re-layouts  7.46 us (2%)
  other arithmetic  3.62 us (1%)
    ppermute x32, starting transfers between devices, shifted(): return lax.ppermute(block, axis, route)  111 us
    dot_general x48, matrix products, apply_panel(): return jnp.einsum('mrs,mcs->mcr', matrix, vector, precision=HIGHEST)  95.8 us
    ppermute x32, waiting for transfers between devices, shifted(): return lax.ppermute(block, axis, route)  86 us
    all_to_all x1, starting transfers between devices, body(): lax.all_to_all(spectrum, 'mode', split_axis=0, concat_axis=1, tiled=True)  9.92 us
    dot_general x1, matrix products, body(): jnp.dot(dft_table, rhs_phys, precision=HIGHEST, preferred_element_type=jn...  7.41 us
  transfers between devices with their start and end apart: 33, of which 31 were waited for; matrix products, arithmetic and copies ran while one was open for 8% of the time, Pallas kernels for 0%

commit v1 on v0

v1 whole, which is shorter than its diff:
```python
import functools
import math

import jax
import jax.numpy as jnp
import numpy as np
from jax import lax
from jax.experimental import pallas as pl
from jax.experimental.pallas import tpu as pltpu
from jax.sharding import PartitionSpec as P

F32 = jnp.float32
BF16 = jnp.bfloat16
HIGH = lax.Precision.HIGH


def split(x):
    hi = x.astype(BF16)
    return hi, (x - hi.astype(F32)).astype(BF16)


def bdot(a, b):
    return jnp.dot(a, b, preferred_element_type=F32)


def mul_split(v, hi, lo):
    vh, vl = split(v)
    return bdot(vh, hi) + (bdot(vl, hi) + bdot(vh, lo))


def mul(a, b):
    return mul_split(a, *split(b))


def wave_square(index, mode_total):
    wave = index.astype(F32) / mode_total
    return 4.0 * wave * wave


def store_split(ref, at, x):
    hi, lo = split(x)
    ref[at + (0,)] = hi
    ref[at + (1,)] = lo


def slab_kernel(radial_ref, stiff_ref, mass_ref, number_ref, band_ref, rs_ref, rts_ref, push_ref, lift_ref, es_ref, ets_ref):
    slabs, n = radial_ref.shape[0], radial_ref.shape[1]
    for j in range(slabs):
        basis = radial_ref[j]
        store_split(rs_ref, (j,), basis)
        store_split(rts_ref, (j,), basis.T)
        for part, face in enumerate((stiff_ref, mass_ref)):
            turned = mul(face[j].T, basis)
            th, tl = split(turned)
            for side in range(2):
                numbers = number_ref[2 * j + side : 2 * j + side + 1, :]
                hot = (lax.broadcasted_iota(jnp.int32, (n, n), 0) == numbers).astype(F32).astype(BF16)
                kt = bdot(hot, th) + bdot(hot, tl)
                for ref, x in ((lift_ref, kt), (push_ref, kt.T)):
                    hi, lo = split(x)
                    ref[j, side, 0, part * n : (part + 1) * n, :] = hi
                    ref[j, side, 1, part * n : (part + 1) * n, :] = lo
        if j > 0:
            for part in range(2):
                band = band_ref[part, j]
                for ref, x in ((es_ref, band), (ets_ref, band.T)):
                    hi, lo = split(x)
                    ref[j - 1, 0, part * n : (part + 1) * n, :] = hi
                    ref[j - 1, 1, part * n : (part + 1) * n, :] = lo


def map_kernel(group, mode_dev, mode_total, panel_ref, band_ref, maps_ref, pts_ref, uts_ref, nts_ref):
    step = pl.program_id(0)
    first = lax.axis_index("mode") * mode_dev + step * group
    slabs = panel_ref.shape[1]
    bands = [[band_ref[p, j] for p in range(2)] for j in range(slabs)]
    turned = [[bands[j][p].T for p in range(2)] for j in range(slabs)]
    for i in range(group):
        lam = wave_square(first + i, mode_total)
        e = [bands[j][0] + lam * bands[j][1] for j in range(slabs)]
        et = [split(turned[j][0] + lam * turned[j][1]) for j in range(slabs)]
        es = [split(x) for x in e]
        pt = []
        for j in range(slabs):
            x = split(panel_ref[i, j].T)
            pts_ref[i, j, 0] = x[0]
            pts_ref[i, j, 1] = x[1]
            pt.append(x)

        def times(a, b):
            return bdot(a[0], b[0]) + (bdot(a[1], b[0]) + bdot(a[0], b[1]))

        ahead = []
        now = None
        for j in range(slabs):
            first_factor = et[0] if j == 0 else split(times(now, et[j]))
            full = -times(first_factor, pt[j])
            now = split(full)
            nts_ref[i, j, 0] = now[0]
            nts_ref[i, j, 1] = now[1]
            ahead.append(now)
        maps_ref[i, 0] = full
        back = []
        now = es[0]
        for j in range(slabs):
            if j > 0:
                now = split(times(es[j], now))
            uts_ref[i, j, 0] = now[0]
            uts_ref[i, j, 1] = now[1]
            back.append(now)
            full = -times(pt[j], now)
            now = split(full)
        maps_ref[i, 1] = full
        cross = times(ahead[0], back[0])
        for j in range(1, slabs):
            cross = cross + times(ahead[j], back[j])
        maps_ref[i, 2] = cross


def solve_kernel(
    mode_axis,
    mode_dev,
    mode_total,
    chips,
    axial_ref,
    couple_ref,
    axial_eig_ref,
    spec_ref,
    radial_eig_ref,
    rs_ref,
    rts_ref,
    push_ref,
    lift_ref,
    es_ref,
    ets_ref,
    maps_ref,
    pts_ref,
    uts_ref,
    nts_ref,
    out_ref,
    modal,
    placed_in,
    x_in,
    x_send,
    push_send,
    pair_maps,
    chip_maps,
    own_maps,
    vec_send,
    pair_vecs,
    chip_vecs,
    own_vecs,
    back_send,
    back_vecs,
    fin_send,
    fin,
    sem_pm,
    sem_cm_s,
    sem_cm_r,
    sem_pl,
    sem_pv,
    sem_cv_s,
    sem_cv_r,
    sem_bk_s,
    sem_bk_r,
    sem_fn,
    sem_x,
):
    slabs, n = rs_ref.shape[0], rs_ref.shape[-1]
    rows = 2 * mode_dev
    half = mode_dev // 2
    inner = axial_ref.shape[0] // slabs
    me = lax.axis_index("elem")
    count = 2 * chips
    core = lax.rem(me, 2)
    chip = me // 2
    other = 1 - core
    partner = 2 * chip + other
    across = lax.rem(me + count - 1 + 2 * core, count)

    barrier = pltpu.get_barrier_semaphore()
    for k in range(1, chips):
        pl.semaphore_signal(barrier, 1, device_id={"elem": 2 * lax.rem(chip + k, chips) + core})
    pl.semaphore_signal(barrier, 1, device_id={"elem": partner})
    pl.semaphore_signal(barrier, 1, device_id={"elem": across})

    def remote(src, dst, send, recv, device):
        return pltpu.make_async_remote_copy(
            src, dst, send, recv, device_id={"elem": device}, device_id_type=pl.DeviceIdType.MESH
        )

    row = lax.broadcasted_iota(jnp.int32, (rows, n), 0)
    lam = wave_square(lax.axis_index("mode") * mode_dev + row // 2, mode_total)

    def banded(v, ref):
        return mul_split(jnp.concatenate([v, lam * v], axis=1), ref[0], ref[1])

    def per_mode(v, ref, *at):
        vh, vl = split(v)
        both = jnp.concatenate([vh, vl], axis=0)
        sides = lax.broadcasted_iota(jnp.int32, (2 * rows, n), 0)
        sides = jnp.where(sides < rows, sides, sides - rows) // 2
        zero = jnp.zeros_like(both)
        total = None
        low = None
        for m in range(mode_dev):
            mine = jnp.where(sides == m, both, zero)
            term = bdot(mine, ref[(m,) + at + (0,)])
            term_low = bdot(mine[:rows], ref[(m,) + at + (1,)])
            total = term if total is None else total + term
            low = term_low if low is None else low + term_low
        return total[:rows] + (total[rows:] + low)

    width = spec_ref.shape[2]
    for t in range(slabs * (inner + 1)):
        pieces = []
        at = t * n
        while at < (t + 1) * n:
            source = at // width
            stop = min((t + 1) * n, (source + 1) * width)
            pieces.append(spec_ref[source, :, at - source * width : stop - source * width])
            at = stop
        modal[t] = pieces[0] if len(pieces) == 1 else jnp.concatenate(pieces, axis=1)

    pl.semaphore_wait(barrier, chips + 1)
    share = remote(
        maps_ref.at[pl.ds(half * other, half)], pair_maps.at[core], sem_pm.at[0], sem_pm.at[1], partner
    )
    share.start()

    spectral = []
    inverses = []
    placed = []
    for j in range(slabs):
        base = j * (inner + 1)
        x = jnp.concatenate([modal[base + a] for a in range(inner)], axis=0)
        x = mul_split(x, rs_ref[j, 0], rs_ref[j, 1])
        values = []
        scales = []
        for b in range(inner):
            total = x[:rows] * axial_ref[j * inner, b]
            for a in range(1, inner):
                total = total + x[a * rows : (a + 1) * rows] * axial_ref[j * inner + a, b]
            scale = 1.0 / (axial_eig_ref[j, b] + radial_eig_ref[j : j + 1, :] + lam)
            scales.append(scale)
            values.append(total * scale)
        spectral.append(values)
        inverses.append(scales)
        sums = [None, None]
        for a in range(inner):
            total = values[0] * axial_ref[j * inner + a, 0]
            for b in range(1, inner):
                total = total + values[b] * axial_ref[j * inner + a, b]
            for side in range(2):
                term = total * couple_ref[2 * j + side, a]
                sums[side] = term if sums[side] is None else sums[side] + term
        placed.append([banded(sums[side], push_ref.at[j, side]) for side in range(2)])
        if j == 0:
            push_send[...] = placed[0][0]

            @pl.when(me > 0)
            def _():
                remote(push_send, placed_in, sem_pl.at[0], sem_pl.at[1], me - 1).start()

    pair_maps[core] = maps_ref[pl.ds(half * core, half)]
    share.wait()
    for i in range(half):
        a0, b0, c0 = (pair_maps[0, i, k] for k in range(3))
        a1, b1, c1 = (pair_maps[1, i, k] for k in range(3))
        a0s, b0s = split(a0), split(b0)
        chip_maps[i, 0] = mul(a0, a1)
        chip_maps[i, 1] = mul_split(b1, *b0s)
        chip_maps[i, 2] = c0 + mul_split(mul(a0, c1), *b0s)
        owner = half * core + i

        @pl.when(owner != chip)
        def _():
            remote(
                chip_maps.at[i], own_maps.at[chip], sem_cm_s.at[i], sem_cm_r.at[chip], 2 * owner + core
            ).start()

        @pl.when(owner == chip)
        def _():
            own_maps[chip] = chip_maps[i]

    loads = [modal[j * (inner + 1) + inner] - placed[j][1] for j in range(slabs)]
    for j in range(slabs - 1):
        loads[j] = loads[j] - placed[j + 1][0]
    local = [per_mode(loads[0], pts_ref, 0)]
    for j in range(1, slabs):
        load = loads[j] - banded(local[j - 1], ets_ref.at[j - 1])
        if j == slabs - 1:

            @pl.when(me == count - 1)
            def _():
                placed_in[...] = jnp.zeros_like(placed_in)

            @pl.when(me < count - 1)
            def _():
                remote(push_send, placed_in, sem_pl.at[0], sem_pl.at[1], me).wait_recv()

            load = load - placed_in[...]
        local.append(per_mode(load, pts_ref, j))
    offset = per_mode(local[0], uts_ref, 0)
    for j in range(1, slabs):
        offset = offset + per_mode(local[j], uts_ref, j)
    vec_send[...] = jnp.zeros_like(vec_send)
    for m in range(mode_dev):
        vec_send[m, 0:2, :] = local[-1][2 * m : 2 * m + 2]
        vec_send[m, 2:4, :] = offset[2 * m : 2 * m + 2]
    swap = remote(
        vec_send.at[pl.ds(half * other, half)], pair_vecs.at[core], sem_pv.at[0], sem_pv.at[1], partner
    )
    swap.start()
    pair_vecs[core] = vec_send[pl.ds(half * core, half)]
    swap.wait()
    low = lax.broadcasted_iota(jnp.int32, (8, n), 0) < 2
    for i in range(half):
        t0, t1 = pair_vecs[0, i], pair_vecs[1, i]
        b0 = pair_maps[0, i, 1]
        a1, c1 = pair_maps[1, i, 0], pair_maps[1, i, 2]
        inside = t1 + pltpu.roll(mul(t0, c1), 2, 0)
        chip_vecs[i] = jnp.where(low, mul(t0, a1) + t1, t0 + mul(inside, b0))
        owner = half * core + i

        @pl.when(owner != chip)
        def _():
            remote(
                chip_vecs.at[i], own_vecs.at[chip], sem_cv_s.at[i], sem_cv_r.at[chip], 2 * owner + core
            ).start()

        @pl.when(owner == chip)
        def _():
            own_vecs[chip] = chip_vecs[i]

    mine = chip - half * core

    @pl.when(chip // half == core)
    def _():
        for z in range(chips):

            @pl.when(z != chip)
            def _():
                remote(chip_maps.at[0], own_maps.at[z], sem_cm_s.at[0], sem_cm_r.at[z], me).wait_recv()
                remote(chip_vecs.at[0], own_vecs.at[z], sem_cv_s.at[0], sem_cv_r.at[z], me).wait_recv()

        state = jnp.zeros((8, n), F32)
        before = []
        terms = []
        for z in range(chips):
            before.append(state)
            if z > 0:
                terms.append(own_vecs[z] + pltpu.roll(mul(state, own_maps[z, 2]), 2, 0))
                state = mul(state, own_maps[z, 0]) + own_vecs[z]
            else:
                terms.append(own_vecs[z])
                state = own_vecs[z]
        state = jnp.zeros((8, n), F32)
        for z in reversed(range(chips)):
            back_send[z] = jnp.where(low, before[z], state)

            @pl.when(z != chip)
            def _():
                remote(back_send.at[z], back_vecs.at[mine], sem_bk_s.at[z], sem_bk_r.at[mine], 2 * z + core).start()

            @pl.when(z == chip)
            def _():
                back_vecs[mine] = back_send[z]

            if z > 0:
                state = terms[z] if z == chips - 1 else mul(state, own_maps[z, 1]) + terms[z]

    for i in range(half):

        @pl.when(half * core + i != chip)
        def _():
            remote(back_send.at[0], back_vecs.at[i], sem_bk_s.at[0], sem_bk_r.at[i], me).wait_recv()

        t0, t1 = pair_vecs[0, i], pair_vecs[1, i]
        a0 = pair_maps[0, i, 0]
        b1, c1 = pair_maps[1, i, 1], pair_maps[1, i, 2]
        ends = back_vecs[i]
        middle = mul(ends, a0) + t0
        turned = mul(ends, b1) + t1 + pltpu.roll(mul(middle, c1), 2, 0)
        for_zero = jnp.where(low, ends, turned)
        for_one = jnp.where(low, middle, ends)
        fin[half * core + i] = jnp.where(core == 0, for_zero, for_one)
        fin_send[i] = jnp.where(core == 0, for_one, for_zero)
    give = remote(fin_send, fin.at[pl.ds(half * core, half)], sem_fn.at[0], sem_fn.at[1], partner)
    give.start()
    give.wait_send()
    remote(fin_send, fin.at[pl.ds(half * other, half)], sem_fn.at[0], sem_fn.at[1], partner).wait_recv()

    start = jnp.concatenate([fin[m, 0:2, :] for m in range(mode_dev)], axis=0)
    end = jnp.concatenate([fin[m, 2:4, :] for m in range(mode_dev)], axis=0)
    values = [None] * slabs
    for j in reversed(range(slabs)):
        full = local[j] + per_mode(start, nts_ref, j)
        values[j] = full - per_mode(end, pts_ref, j)
        if j == slabs - 1:
            x_send[...] = values[j]

            @pl.when(me < count - 1)
            def _():
                remote(x_send, x_in, sem_x.at[0], sem_x.at[1], me + 1).start()

        if j > 0:
            end = banded(values[j], es_ref.at[j - 1])

    for j in reversed(range(slabs)):
        if j == 0:

            @pl.when(me == 0)
            def _():
                x_in[...] = jnp.zeros_like(x_in)

            @pl.when(me > 0)
            def _():
                remote(x_send, x_in, sem_x.at[0], sem_x.at[1], me).wait_recv()

            faces = [x_in[...], values[0]]
        else:
            faces = [values[j - 1], values[j]]
        lifted = [banded(faces[side], lift_ref.at[j, side]) for side in range(2)]
        spread = [
            lifted[0] * couple_ref[2 * j, a] + lifted[1] * couple_ref[2 * j + 1, a] for a in range(inner)
        ]
        left = []
        for b in range(inner):
            total = spread[0] * axial_ref[j * inner, b]
            for a in range(1, inner):
                total = total + spread[a] * axial_ref[j * inner + a, b]
            left.append(spectral[j][b] - total * inverses[j][b])
        turned = []
        for a in range(inner):
            total = left[0] * axial_ref[j * inner + a, 0]
            for b in range(1, inner):
                total = total + left[b] * axial_ref[j * inner + a, b]
            turned.append(total)
        result = mul_split(jnp.concatenate(turned, axis=0), rts_ref[j, 0], rts_ref[j, 1])
        base = j * (inner + 1) * n
        for a in range(inner):
            out_ref[:, base + a * n : base + (a + 1) * n] = result[a * rows : (a + 1) * rows]
        out_ref[:, base + inner * n : base + (inner + 1) * n] = values[j]

    @pl.when(me > 0)
    def _():
        remote(push_send, placed_in, sem_pl.at[0], sem_pl.at[1], me - 1).wait_send()

    @pl.when(me < count - 1)
    def _():
        remote(x_send, x_in, sem_x.at[0], sem_x.at[1], me + 1).wait_send()

    for i in range(half):

        @pl.when(half * core + i != chip)
        def _():
            owner = 2 * (half * core + i) + core
            remote(chip_maps.at[i], own_maps.at[chip], sem_cm_s.at[i], sem_cm_r.at[chip], owner).wait_send()
            remote(chip_vecs.at[i], own_vecs.at[chip], sem_cv_s.at[i], sem_cv_r.at[chip], owner).wait_send()

    @pl.when(chip // half == core)
    def _():
        for z in range(chips):

            @pl.when(z != chip)
            def _():
                remote(back_send.at[z], back_vecs.at[mine], sem_bk_s.at[z], sem_bk_r.at[mine], 2 * z + core).wait_send()


def fourier_table(planes):
    row = np.arange(planes)[:, None]
    angles = (row // 2 * np.arange(planes)[None, :] % planes) * (2.0 * math.pi / planes)
    return (np.where(row % 2 == 0, np.cos(angles), -np.sin(angles)) / math.sqrt(planes)).astype(np.float32)


VMEM = pl.BlockSpec(memory_space=pltpu.VMEM)
SMEM = pl.BlockSpec(memory_space=pltpu.SMEM)


def body(
    rhs_phys,
    radial_basis,
    axial_basis,
    radial_eig,
    axial_eig,
    face_stiff,
    face_mass,
    axial_coupling,
    face_numbering,
    band_panels,
    inverse_panels,
):
    planes = rhs_phys.shape[0]
    mode_dev, slabs, n = inverse_panels.shape[:3]
    inner = axial_basis.shape[1]
    mode_axis = lax.axis_size("mode")
    chips = lax.axis_size("elem") // 2
    mode_total = mode_dev * mode_axis
    rows = 2 * mode_dev
    half = mode_dev // 2
    S = jax.ShapeDtypeStruct

    spectrum = jnp.dot(jnp.asarray(fourier_table(planes)), rhs_phys, precision=HIGH, preferred_element_type=F32)
    spectrum = lax.all_to_all(spectrum.reshape(mode_axis, rows, -1), "mode", split_axis=0, concat_axis=0)

    rs, rts, push, lift, es, ets = pl.pallas_call(
        slab_kernel,
        out_shape=[
            S((slabs, 2, n, n), BF16),
            S((slabs, 2, n, n), BF16),
            S((slabs, 2, 2, 2 * n, n), BF16),
            S((slabs, 2, 2, 2 * n, n), BF16),
            S((slabs - 1, 2, 2 * n, n), BF16),
            S((slabs - 1, 2, 2 * n, n), BF16),
        ],
        in_specs=[VMEM] * 5,
        out_specs=[VMEM] * 6,
        compiler_params=pltpu.CompilerParams(vmem_limit_bytes=32 << 20),
        name="slab_maps",
    )(radial_basis, face_stiff, face_mass, face_numbering.reshape(2 * slabs, n), band_panels)

    group = min(GROUP, mode_dev)
    maps, pts, uts, nts = pl.pallas_call(
        functools.partial(map_kernel, group, mode_dev, mode_total),
        grid=(mode_dev // group,),
        out_shape=[
            S((mode_dev, 3, n, n), F32),
            S((mode_dev, slabs, 2, n, n), BF16),
            S((mode_dev, slabs, 2, n, n), BF16),
            S((mode_dev, slabs, 2, n, n), BF16),
        ],
        in_specs=[
            pl.BlockSpec((group, slabs, n, n), lambda i: (i, 0, 0, 0)),
            pl.BlockSpec((2, slabs, n, n), lambda i: (0, 0, 0, 0)),
        ],
        out_specs=[
            pl.BlockSpec((group, 3, n, n), lambda i: (i, 0, 0, 0)),
            pl.BlockSpec((group, slabs, 2, n, n), lambda i: (i, 0, 0, 0, 0)),
            pl.BlockSpec((group, slabs, 2, n, n), lambda i: (i, 0, 0, 0, 0)),
            pl.BlockSpec((group, slabs, 2, n, n), lambda i: (i, 0, 0, 0, 0)),
        ],
        compiler_params=pltpu.CompilerParams(vmem_limit_bytes=32 << 20),
        name="mode_maps",
    )(inverse_panels, band_panels)

    V = pltpu.VMEM
    D = pltpu.SemaphoreType.DMA
    return pl.pallas_call(
        functools.partial(solve_kernel, mode_axis, mode_dev, mode_total, chips),
        out_shape=S((rows, slabs * (inner + 1) * n), F32),
        in_specs=[SMEM] * 3 + [VMEM] * 12,
        out_specs=VMEM,
        scratch_shapes=[
            V((slabs * (inner + 1), rows, n), F32),
            V((rows, n), F32),
            V((rows, n), F32),
            V((rows, n), F32),
            V((rows, n), F32),
            V((2, half, 3, n, n), F32),
            V((half, 3, n, n), F32),
            V((chips, 3, n, n), F32),
            V((mode_dev, 8, n), F32),
            V((2, half, 8, n), F32),
            V((half, 8, n), F32),
            V((chips, 8, n), F32),
            V((chips, 8, n), F32),
            V((half, 8, n), F32),
            V((half, 8, n), F32),
            V((mode_dev, 8, n), F32),
            D((2,)),
            D((half,)),
            D((chips,)),
            D((2,)),
            D((2,)),
            D((half,)),
            D((chips,)),
            D((chips,)),
            D((half,)),
            D((2,)),
            D((2,)),
        ],
        compiler_params=pltpu.CompilerParams(
            collective_id=0, has_side_effects=True, vmem_limit_bytes=48 << 20
        ),
        name="slab_solve",
    )(
        axial_basis.reshape(slabs * inner, inner),
        axial_coupling.reshape(2 * slabs, inner),
        axial_eig,
        spectrum,
        radial_eig,
        rs,
        rts,
        push,
        lift,
        es,
        ets,
        maps,
        pts,
        uts,
        nts,
    )


GROUP = 4


def solution(mesh):
    placed = (
        P(None, ("elem", "mode")),
        P("elem", None, None),
        P("elem", None, None),
        P("elem", None),
        P("elem", None),
        P("elem", None, None),
        P("elem", None, None),
        P("elem", None, None),
        P("elem", None, None),
        P(None, "elem", None, None),
        P("mode", "elem", None, None),
    )
    return jax.shard_map(
        body, mesh=mesh, in_specs=placed, out_specs=P("mode", "elem"), check_vma=False
    )
```

time: 353 us -> 86 us (0.24)
  the two profiles are of different devices: /device:TPU:195 before, /device:TPU:1 now
where the time goes in v1:
time: 86 us; the launch traced here: 85.6 us
  Pallas kernels  58.1 us (68%)
  local copies, waits for them, and re-layouts  14.2 us (17%)
  starting transfers between devices  10.6 us (12%)
  matrix products  2.51 us (3%)
    pallas_call x1, Pallas kernels, body(): pl.pallas_call(functools.partial(solve_kernel, mode_axis, mode_dev, mode_...  45.9 us
    unnamed x45, local copies, waits for them, and re-layouts  13.6 us
    pallas_call x1, Pallas kernels, body(): pl.pallas_call(functools.partial(map_kernel, group, mode_dev, mode_total)...  10.7 us
    all_to_all x1, starting transfers between devices, body(): lax.all_to_all(spectrum.reshape(mode_axis, rows, -1), 'mode', split_axis=...  10.6 us
    dot_general x1, matrix products, body(): jnp.dot(jnp.asarray(fourier_table(planes)), rhs_phys, precision=HIGH, pre...  2.51 us
  transfers between devices with their start and end apart: 1, of which 0 were waited for; matrix products, arithmetic and copies ran while one was open for 1% of the time, Pallas kernels for 14%

profile of v1, /device:TPU:1, one launch (start us, length us, event | category | flops | bytes accessed | tf_op | source)
XLA Modules:
  0.0 85.6 jit_solution(7360115494130015715)
XLA Ops:
  0.0 0.0 copy-start
  0.0 0.0 copy-start.20
  0.0 0.0 copy-start.21
  0.0 0.0 copy-start.19
  0.0 0.0 copy-start.2
  0.0 0.0 copy-start.1
  0.0 0.9 %copy-done = f32[512,96]{0,1:T(8,128)S(1)} copy-done((f32[512,96]{0,1:T(8,128)S(1)}, f32[512,96]{0,1:T(8,128)}, u32[]{:S(2)}) %copy-start) | copy-done | bytes 196632
  0.9 2.5 %fusion = f32[512,96]{1,0:T(8,128)} fusion(f32[512,512]{1,0:T(8,128)} %constant.2.clone, f32[512,96]{0,1:T(8,128)S(1)} %copy-done), kind=kOutput, calls=%fused_computation | convolution fusion | flops 150994944 | bytes 1441792 | tf_op jit(solution)/shard_map/dot_general | solution.py:504
  3.4 0.0 copy-start.9
  3.4 0.0 copy-start.10
  3.4 0.0 copy-start.11
  3.4 10.6 %all-to-all-start = ((f32[32,16,96]{2,1,0:T(8,128)}), f32[32,16,96]{2,1,0:T(8,128)S(1)}, u32[]{:S(2)}, u32[]{:S(2)}) async-start(f32[32,16,96]{2,1,0:T(8,128)} %bitcast), calls=%async_computation | async-start | bytes 524288 | tf_op jit(solution)/shard_map/all_to_all | solution.py:505
  14.1 0.0 copy-done.20
  14.1 0.0 copy-done.21
  14.1 0.6 reshape.15.number_ref
  14.7 0.0 copy-done.19
  14.7 0.0 copy-done.2
  14.7 0.0 copy-done.1
  14.7 0.0 copy-start.16
  14.8 10.7 %mode_maps.1 = (f32[8,3,128,128]{3,2,1,0:T(8,128)S(1)}, bf16[8,3,2,128,128]{4,3,2,1,0:T(8,128)(2,1)S(1)}, bf16[8,3,2,128,128]{4,3,2,1,0:T(8,128)(2,1)S(1)}, bf16[8,3,2,128,128]{4,3,2,1,0:T(8,128)(2,1)S(1)}) custom-call(f32[8,3,128,128]{3,2,1,0:T(8,128)S(1)} %copy-done.1, f32[2,3,128,128]{3,2,1,0:T(8,128)S(1)} %copy-done.2), custom_call_target="tpu_custom_call" | custom-call | tf_op jit(solution)/shard_map/mode_maps/pallas_call | solution.py:524
  25.5 0.0 copy-start.3
  25.5 1.2 %copy-done.3 = f32[8,3,128,128]{3,2,1,0:T(8,128)} copy-done((f32[8,3,128,128]{3,2,1,0:T(8,128)}, f32[8,3,128,128]{3,2,1,0:T(8,128)S(1)}, u32[]{:S(2)}) %copy-start.3) | copy-done | bytes 1572888
  26.7 0.0 copy-start.5
  26.7 1.2 %copy-done.5 = bf16[8,3,2,128,128]{4,3,2,1,0:T(8,128)(2,1)} copy-done((bf16[8,3,2,128,128]{4,3,2,1,0:T(8,128)(2,1)}, bf16[8,3,2,128,128]{4,3,2,1,0:T(8,128)(2,1)S(1)}, u32[]{:S(2)}) %copy-start.5) | copy-done | bytes 1572888
  27.9 0.0 copy-start.7
  27.9 1.2 %copy-done.7 = bf16[8,3,2,128,128]{4,3,2,1,0:T(8,128)(2,1)} copy-done((bf16[8,3,2,128,128]{4,3,2,1,0:T(8,128)(2,1)}, bf16[8,3,2,128,128]{4,3,2,1,0:T(8,128)(2,1)S(1)}, u32[]{:S(2)}) %copy-start.7) | copy-done | bytes 1572888
  29.0 0.0 copy-start.8
  29.0 1.1 %copy-done.8 = bf16[8,3,2,128,128]{4,3,2,1,0:T(8,128)(2,1)} copy-done((bf16[8,3,2,128,128]{4,3,2,1,0:T(8,128)(2,1)}, bf16[8,3,2,128,128]{4,3,2,1,0:T(8,128)(2,1)S(1)}, u32[]{:S(2)}) %copy-start.8) | copy-done | bytes 1572888
  30.2 0.0 copy-done.9
  30.2 0.0 copy-done.10
  30.2 0.0 copy-done.11
  30.2 0.0 copy-done.16
  30.2 1.4 %slab_maps.1 = (bf16[3,2,128,128]{3,2,1,0:T(8,128)(2,1)S(1)}, bf16[3,2,128,128]{3,2,1,0:T(8,128)(2,1)S(1)}, bf16[3,2,2,256,128]{4,3,2,1,0:T(8,128)(2,1)S(1)}, bf...) custom-call(f32[3,128,128]{2,1,0:T(8,128)S(1)} %copy-done.9, ...), custom_call_target="tpu_custom_call" | custom-call | tf_op jit(solution)/shard_map/slab_maps/pallas_call | solution.py:507
  31.6 0.0 copy-start.12
  31.7 0.7 copy-done.12
  32.3 0.0 copy-start.14
  32.3 0.7 copy-done.14
  33.0 0.0 all-to-all-done.spec_ref
  33.0 0.0 copy-start.4
  33.0 1.4 %copy-done.4 = f32[8,3,128,128]{3,2,1,0:T(8,128)S(1)} copy-done((f32[8,3,128,128]{3,2,1,0:T(8,128)S(1)}, f32[8,3,128,128]{3,2,1,0:T(8,128)}, u32[]{:S(2)}) %copy-start.4) | copy-done | bytes 1572888
  34.4 0.0 copy-start.6
  34.4 1.4 %copy-done.6 = bf16[8,3,2,128,128]{4,3,2,1,0:T(8,128)(2,1)S(1)} copy-done((bf16[8,3,2,128,128]{4,3,2,1,0:T(8,128)(2,1)S(1)}, bf16[8,3,2,128,128]{4,3,2,1,0:T(8,128)(2,1)}, u32[]{:S(2)}) %copy-start.6) | copy-done | bytes 1572888
  35.8 0.0 copy-start.13
  35.8 0.9 %copy-done.13 = bf16[3,2,128,128]{3,2,1,0:T(8,128)(2,1)S(1)} copy-done((bf16[3,2,128,128]{3,2,1,0:T(8,128)(2,1)S(1)}, bf16[3,2,128,128]{3,2,1,0:T(8,128)(2,1)}, u32[]{:S(2)}) %copy-start.13) | copy-done | bytes 196632
  36.7 0.0 copy-start.15
  36.7 0.9 %copy-done.15 = bf16[3,2,128,128]{3,2,1,0:T(8,128)(2,1)S(1)} copy-done((bf16[3,2,128,128]{3,2,1,0:T(8,128)(2,1)S(1)}, bf16[3,2,128,128]{3,2,1,0:T(8,128)(2,1)}, u32[]{:S(2)}) %copy-start.15) | copy-done | bytes 196632
  37.7 0.0 copy-start.17
  37.7 0.7 copy-done.17
  38.3 0.0 copy-start.18
  38.4 0.7 copy-done.18
  39.0 45.9 %slab_solve.1 = f32[16,3072]{1,0:T(8,128)S(1)} custom-call(f32[21,7]{1,0:T(8,128)S(1)} %reshape.16.axial_ref, f32[6,7]{1,0:T(8,128)S(1)} %reshape.13.couple_ref, f32[3,7]{1,0:T(4,128)S(1)} %copy-done.17, f32[32,16,96]{2,1,0:T(8,128)S(1)} %all-to-all-done.spec_ref, f32[3,128]{1,0:T(4,128)S(1)} %copy-done.18, bf16[3,2,128,128]{3,2,1,0:T(8,128)(2,1)S(1)} %copy-done.13, ...), custom_call_target="tpu_custom_call" | custom-call | tf_op jit(solution)/shard_map/slab_solve/pallas_call | solution.py:549
  84.9 0.7 copy.20
  (2 shorter events, 0.0 us)
Async XLA Ops:
  0.0 0.9 %copy-start = (f32[512,96]{0,1:T(8,128)S(1)}, f32[512,96]{0,1:T(8,128)}, u32[]{:S(2)}) copy-start(f32[512,96]{0,1:T(8,128)} %param.12) | copy-start | bytes 589828
  0.0 14.1 %copy-start.20 = (f32[3,2,7]{2,1,0:T(2,128)S(1)}, f32[3,2,7]{2,1,0:T(2,128)}, u32[]{:S(2)}) copy-start(f32[3,2,7]{2,1,0:T(2,128)} %param.19) | copy-start | bytes 508
  0.0 14.1 %copy-start.21 = (s32[3,2,128]{2,1,0:T(2,128)S(1)}, s32[3,2,128]{2,1,0:T(2,128)}, u32[]{:S(2)}) copy-start(s32[3,2,128]{2,1,0:T(2,128)} %param.20) | copy-start | bytes 9220
  0.0 14.7 %copy-start.19 = (f32[3,7,7]{2,1,0:T(8,128)S(1)}, f32[3,7,7]{2,1,0:T(8,128)}, u32[]{:S(2)}) copy-start(f32[3,7,7]{2,1,0:T(8,128)} %param.14) | copy-start | bytes 1768
  0.0 14.7 %copy-start.2 = (f32[2,3,128,128]{3,2,1,0:T(8,128)S(1)}, f32[2,3,128,128]{3,2,1,0:T(8,128)}, u32[]{:S(2)}) copy-start(f32[2,3,128,128]{3,2,1,0:T(8,128)} %band_ref.3) | copy-start | bytes 1179652
  0.0 14.7 %copy-start.1 = (f32[8,3,128,128]{3,2,1,0:T(8,128)S(1)}, f32[8,3,128,128]{3,2,1,0:T(8,128)}, u32[]{:S(2)}) copy-start(f32[8,3,128,128]{3,2,1,0:T(8,128)} %panel_ref.1) | copy-start | bytes 4718596
  3.4 26.7 %copy-start.9 = (f32[3,128,128]{2,1,0:T(8,128)S(1)}, f32[3,128,128]{2,1,0:T(8,128)}, u32[]{:S(2)}) copy-start(f32[3,128,128]{2,1,0:T(8,128)} %radial_ref.1) | copy-start | bytes 589828
  3.4 26.7 %copy-start.10 = (f32[3,128,128]{2,1,0:T(8,128)S(1)}, f32[3,128,128]{2,1,0:T(8,128)}, u32[]{:S(2)}) copy-start(f32[3,128,128]{2,1,0:T(8,128)} %stiff_ref.1) | copy-start | bytes 589828
  3.4 26.7 %copy-start.11 = (f32[3,128,128]{2,1,0:T(8,128)S(1)}, f32[3,128,128]{2,1,0:T(8,128)}, u32[]{:S(2)}) copy-start(f32[3,128,128]{2,1,0:T(8,128)} %mass_ref.1) | copy-start | bytes 589828
  3.4 29.5 %all-to-all-start = ((f32[32,16,96]{2,1,0:T(8,128)}), f32[32,16,96]{2,1,0:T(8,128)S(1)}, u32[]{:S(2)}, u32[]{:S(2)}) async-start(f32[32,16,96]{2,1,0:T(8,128)} %bitcast), calls=%async_computation | async-start | bytes 524288 | tf_op jit(solution)/shard_map/all_to_all | solution.py:505
  14.7 15.4 %copy-start.16 = (s32[6,128]{1,0:T(8,128)S(1)}, s32[6,128]{1,0:T(8,128)}, u32[]{:S(2)}) copy-start(s32[6,128]{1,0:T(8,128)} %reshape.15.number_ref) | copy-start | bytes 9220
  25.5 1.2 %copy-start.3 = (f32[8,3,128,128]{3,2,1,0:T(8,128)}, f32[8,3,128,128]{3,2,1,0:T(8,128)S(1)}, u32[]{:S(2)}) copy-start(f32[8,3,128,128]{3,2,1,0:T(8,128)S(1)} %get-tuple-element.21.maps_ref) | copy-start | bytes 4718596
  26.7 1.2 %copy-start.5 = (bf16[8,3,2,128,128]{4,3,2,1,0:T(8,128)(2,1)}, bf16[8,3,2,128,128]{4,3,2,1,0:T(8,128)(2,1)S(1)}, u32[]{:S(2)}) copy-start(bf16[8,3,2,128,128]{4,3,2,1,0:T(8,128)(2,1)S(1)} %get-tuple-element.22.pts_ref) | copy-start | bytes 4718596
  27.9 1.2 %copy-start.7 = (bf16[8,3,2,128,128]{4,3,2,1,0:T(8,128)(2,1)}, bf16[8,3,2,128,128]{4,3,2,1,0:T(8,128)(2,1)S(1)}, u32[]{:S(2)}) copy-start(bf16[8,3,2,128,128]{4,3,2,1,0:T(8,128)(2,1)S(1)} %get-tuple-element.23.uts_ref) | copy-start | bytes 4718596
  29.0 1.1 %copy-start.8 = (bf16[8,3,2,128,128]{4,3,2,1,0:T(8,128)(2,1)}, bf16[8,3,2,128,128]{4,3,2,1,0:T(8,128)(2,1)S(1)}, u32[]{:S(2)}) copy-start(bf16[8,3,2,128,128]{4,3,2,1,0:T(8,128)(2,1)S(1)} %get-tuple-element.24.nts_ref) | copy-start | bytes 4718596
  31.6 0.7 copy-start.12
  32.3 0.7 copy-start.14
  33.0 1.4 %copy-start.4 = (f32[8,3,128,128]{3,2,1,0:T(8,128)S(1)}, f32[8,3,128,128]{3,2,1,0:T(8,128)}, u32[]{:S(2)}) copy-start(f32[8,3,128,128]{3,2,1,0:T(8,128)} %copy-done.3) | copy-start | bytes 4718596
  34.4 1.4 %copy-start.6 = (bf16[8,3,2,128,128]{4,3,2,1,0:T(8,128)(2,1)S(1)}, bf16[8,3,2,128,128]{4,3,2,1,0:T(8,128)(2,1)}, u32[]{:S(2)}) copy-start(bf16[8,3,2,128,128]{4,3,2,1,0:T(8,128)(2,1)} %copy-done.5) | copy-start | bytes 4718596
  35.8 0.9 %copy-start.13 = (bf16[3,2,128,128]{3,2,1,0:T(8,128)(2,1)S(1)}, bf16[3,2,128,128]{3,2,1,0:T(8,128)(2,1)}, u32[]{:S(2)}) copy-start(bf16[3,2,128,128]{3,2,1,0:T(8,128)(2,1)} %copy-done.12) | copy-start | bytes 589828
  36.7 0.9 %copy-start.15 = (bf16[3,2,128,128]{3,2,1,0:T(8,128)(2,1)S(1)}, bf16[3,2,128,128]{3,2,1,0:T(8,128)(2,1)}, u32[]{:S(2)}) copy-start(bf16[3,2,128,128]{3,2,1,0:T(8,128)(2,1)} %copy-done.14) | copy-start | bytes 589828
  37.7 0.7 copy-start.17
  38.3 0.7 copy-start.18

commit v2 on v1

v2 whole, which is shorter than its diff:
```python
import functools
import math
from types import SimpleNamespace

import jax
import jax.numpy as jnp
import ml_dtypes
import numpy as np
from jax import lax
from jax.experimental import pallas as pl
from jax.experimental.pallas import tpu as pltpu
from jax.sharding import PartitionSpec as P

F32 = jnp.float32
BF16 = jnp.bfloat16
HIGH = lax.Precision.HIGH


def split(x):
    hi = x.astype(BF16)
    return hi, (x - hi.astype(F32)).astype(BF16)


def bdot(a, b):
    return jnp.dot(a, b, preferred_element_type=F32)


def mul_split(v, hi, lo):
    vh, vl = split(v)
    return bdot(vh, hi) + (bdot(vl, hi) + bdot(vh, lo))


def mul(a, b):
    return mul_split(a, *split(b))


def wave_square(index, mode_total):
    wave = index.astype(F32) / mode_total
    return 4.0 * wave * wave


def store_split(ref, at, x):
    hi, lo = split(x)
    ref[at + (0,)] = hi
    ref[at + (1,)] = lo


def slab_matrices(s, number_ref):
    slabs, n = s.radial.shape[0], s.radial.shape[1]
    turned = []
    for j in range(slabs):
        basis = s.radial[j]
        store_split(s.rs, (j,), basis)
        store_split(s.rts, (j,), basis.T)
        for face in (s.stiff, s.mass):
            turned.append(split(mul(face[j].T, basis)))
    for j in range(slabs):
        for side in range(2):
            numbers = number_ref[2 * j + side : 2 * j + side + 1, :]
            hot = (lax.broadcasted_iota(jnp.int32, (n, n), 0) == numbers).astype(F32).astype(BF16)
            for part in range(2):
                th, tl = turned[2 * j + part]
                kt = bdot(hot, th) + bdot(hot, tl)
                for ref, x in ((s.lift, kt), (s.push, kt.T)):
                    hi, lo = split(x)
                    ref[j, side, 0, part * n : (part + 1) * n, :] = hi
                    ref[j, side, 1, part * n : (part + 1) * n, :] = lo
    for j in range(1, slabs):
        for part in range(2):
            band = s.band[part, j]
            for ref, x in ((s.es, band), (s.ets, band.T)):
                hi, lo = split(x)
                ref[j - 1, 0, part * n : (part + 1) * n, :] = hi
                ref[j - 1, 1, part * n : (part + 1) * n, :] = lo


def times(a, b):
    return bdot(a[0], b[0]) + (bdot(a[1], b[0]) + bdot(a[0], b[1]))


def mode_maps(s, modes, first, mode_total):
    slabs = s.panel.shape[1]
    count = len(modes)
    turned = [[s.band[p, j].T for p in range(2)] for j in range(slabs)]
    lams = [wave_square(first + m, mode_total) for m in modes]
    es = [[split(s.band[0, j] + lam * s.band[1, j]) for j in range(slabs)] for lam in lams]
    ets = [[split(turned[j][0] + lam * turned[j][1]) for j in range(slabs)] for lam in lams]
    pts = [[split(s.panel[m, j].T) for j in range(slabs)] for m in modes]
    for i, m in enumerate(modes):
        for j in range(slabs):
            s.pts[m, j, 0] = pts[i][j][0]
            s.pts[m, j, 1] = pts[i][j][1]
    ahead = [ets[i][0] for i in range(count)]
    back = [es[i][0] for i in range(count)]
    cross = [None] * count
    nears = [[] for _ in modes]
    for j in range(slabs):
        if j > 0:
            for i in range(count):
                ahead[i] = split(times(ahead[i], ets[i][j]))
                back[i] = split(times(es[i][j], back[i]))
        for i, m in enumerate(modes):
            s.uts[m, j, 0] = back[i][0]
            s.uts[m, j, 1] = back[i][1]
            full = -times(ahead[i], pts[i][j])
            ahead[i] = split(full)
            s.nts[m, j, 0] = ahead[i][0]
            s.nts[m, j, 1] = ahead[i][1]
            nears[i].append((ahead[i], back[i]))
            backed = -times(pts[i][j], back[i])
            back[i] = split(backed)
            if j == slabs - 1:
                s.maps[m, 0] = full
                s.maps[m, 1] = backed
    for j in range(slabs):
        for i in range(count):
            term = times(*nears[i][j])
            cross[i] = term if cross[i] is None else cross[i] + term
    for i, m in enumerate(modes):
        s.maps[m, 2] = cross[i]


def solve_kernel(
    names,
    mode_axis,
    mode_dev,
    mode_total,
    chips,
    axial_ref,
    couple_ref,
    axial_eig_ref,
    radial_eig_ref,
    number_ref,
    *refs,
):
    s = SimpleNamespace(**dict(zip(names, refs)))
    out_ref = s.out
    slabs, n = s.rs.shape[0], s.rs.shape[-1]
    rows = 2 * mode_dev
    half = mode_dev // 2
    inner = axial_ref.shape[0] // slabs
    me = lax.axis_index("elem")
    count = 2 * chips
    core = lax.rem(me, 2)
    chip = me // 2
    other = 1 - core
    partner = 2 * chip + other
    across = lax.rem(me + count - 1 + 2 * core, count)

    fetch = []
    for at, name in enumerate(LOADED):
        copy = pltpu.make_async_copy(getattr(s, name + "_hbm"), getattr(s, name), s.sem_in.at[at])
        copy.start()
        fetch.append(copy)

    barrier = pltpu.get_barrier_semaphore()
    line = lax.axis_index("mode")
    for k in range(1, mode_axis):
        pl.semaphore_signal(barrier, 1, device_id={"mode": lax.rem(line + k, mode_axis)})
    for k in range(1, chips):
        pl.semaphore_signal(barrier, 1, device_id={"elem": 2 * lax.rem(chip + k, chips) + core})
    pl.semaphore_signal(barrier, 1, device_id={"elem": partner})
    pl.semaphore_signal(barrier, 1, device_id={"elem": across})

    def remote(src, dst, send, recv, device):
        return pltpu.make_async_remote_copy(
            src, dst, send, recv, device_id={"elem": device}, device_id_type=pl.DeviceIdType.MESH
        )

    row = lax.broadcasted_iota(jnp.int32, (rows, n), 0)
    lam = wave_square(lax.axis_index("mode") * mode_dev + row // 2, mode_total)

    def banded(v, ref):
        return mul_split(jnp.concatenate([v, lam * v], axis=1), ref[0], ref[1])

    def per_mode(v, ref, *at):
        vh, vl = split(v)
        both = jnp.concatenate([vh, vl], axis=0)
        sides = lax.broadcasted_iota(jnp.int32, (2 * rows, n), 0)
        sides = jnp.where(sides < rows, sides, sides - rows) // 2
        zero = jnp.zeros_like(both)
        total = None
        low = None
        for m in range(mode_dev):
            mine = jnp.where(sides == m, both, zero)
            term = bdot(mine, ref[(m,) + at + (0,)])
            term_low = bdot(mine[:rows], ref[(m,) + at + (1,)])
            total = term if total is None else total + term
            low = term_low if low is None else low + term_low
        return total[:rows] + (total[rows:] + low)

    for copy in fetch[:2]:
        copy.wait()
    rhs = split(s.rhs[...])
    spectrum = bdot(s.table[0], rhs[0]) + (bdot(s.table[1], rhs[0]) + bdot(s.table[0], rhs[1]))
    s.spec_out[...] = spectrum.reshape(s.spec_out.shape)
    for copy in fetch[2:4]:
        copy.wait()
    first = line * mode_dev
    quarter = max(half // 2, 1)
    parts = [range(at, min(at + quarter, half)) for at in range(0, half, quarter)]
    pl.semaphore_wait(barrier, mode_axis + chips)

    def spread_out(k, carry):
        to = lax.rem(line + k, mode_axis)
        pltpu.make_async_remote_copy(
            s.spec_out.at[to],
            s.spec_in.at[line],
            s.sem_sp.at[0],
            s.sem_sp.at[1],
            device_id={"mode": to},
            device_id_type=pl.DeviceIdType.MESH,
        ).start()
        return carry

    lax.fori_loop(1, mode_axis, spread_out, 0)
    s.spec_in[line] = s.spec_out[line]

    shares = []
    for at, part in enumerate(parts):
        modes = [half * other + i for i in part] + [half * core + i for i in part]
        mode_maps(s, modes, first, mode_total)
        share = remote(
            s.maps.at[pl.ds(half * other + part[0], len(part))],
            s.pair_maps.at[core, pl.ds(part[0], len(part))],
            s.sem_pm_s.at[at],
            s.sem_pm_r.at[at],
            partner,
        )
        share.start()
        shares.append(share)

    s.pair_maps[core] = s.maps[pl.ds(half * core, half)]

    def send_map(i, start):
        owner = half * core + i
        away = jnp.logical_and(owner != chip, chip > 0)
        to = 2 * owner + core
        ends = remote(
            s.chip_maps.at[i, pl.ds(0, 2)],
            s.own_maps.at[chip, pl.ds(0, 2)],
            s.sem_cm_s.at[i, 0],
            s.sem_cm_r.at[chip, 0],
            to,
        )
        cross = remote(
            s.chip_maps.at[i, 2], s.own_maps.at[chip, 2], s.sem_cm_s.at[i, 1], s.sem_cm_r.at[chip, 1], to
        )

        @pl.when(jnp.logical_and(away, chip < chips - 1))
        def _():
            ends.start() if start else ends.wait_send()

        @pl.when(away)
        def _():
            cross.start() if start else cross.wait_send()

    for part, share in zip(parts, shares):
        share.wait()
        pair = [[[split(s.pair_maps[c, i, k]) for k in range(3)] for c in range(2)] for i in part]
        ahead = [times(one[0][0], one[1][0]) for one in pair]
        back = [times(one[1][1], one[0][1]) for one in pair]
        cross = [split(times(one[0][0], one[1][2])) for one in pair]
        cross = [times(x, one[0][1]) for x, one in zip(cross, pair)]
        for at, i in enumerate(part):
            s.chip_maps[i, 0] = ahead[at]
            s.chip_maps[i, 1] = back[at]
            s.chip_maps[i, 2] = s.pair_maps[0, i, 2] + cross[at]
        for i in part:
            send_map(i, True)

            @pl.when(half * core + i == chip)
            def _():
                s.own_maps[chip] = s.chip_maps[i]

    for copy in fetch[4:]:
        copy.wait()
    slab_matrices(s, number_ref)

    others = s.spec_in.at[pl.ds(0, mode_axis - 1)]
    pltpu.make_async_remote_copy(
        others, others, s.sem_sp.at[0], s.sem_sp.at[1], device_id={"mode": line}, device_id_type=pl.DeviceIdType.MESH
    ).wait()
    width = s.spec_in.shape[2]
    modal = []
    for t in range(slabs * (inner + 1)):
        pieces = []
        at = t * n
        while at < (t + 1) * n:
            source = at // width
            stop = min((t + 1) * n, (source + 1) * width)
            pieces.append(s.spec_in[source, :, at - source * width : stop - source * width])
            at = stop
        modal.append(pieces[0] if len(pieces) == 1 else jnp.concatenate(pieces, axis=1))

    spectral = []
    inverses = []
    sums = []
    fields = []
    for j in range(slabs):
        base = j * (inner + 1)
        x = jnp.concatenate([modal[base + a] for a in range(inner)], axis=0)
        fields.append(mul_split(x, s.rs[j, 0], s.rs[j, 1]))
    for j in range(slabs):
        x = fields[j]
        values = []
        scales = []
        for b in range(inner):
            total = x[:rows] * axial_ref[j * inner, b]
            for a in range(1, inner):
                total = total + x[a * rows : (a + 1) * rows] * axial_ref[j * inner + a, b]
            scale = 1.0 / (axial_eig_ref[j, b] + radial_eig_ref[j : j + 1, :] + lam)
            scales.append(scale)
            values.append(total * scale)
        spectral.append(values)
        inverses.append(scales)
        faces = [None, None]
        for a in range(inner):
            total = values[0] * axial_ref[j * inner + a, 0]
            for b in range(1, inner):
                total = total + values[b] * axial_ref[j * inner + a, b]
            for side in range(2):
                term = total * couple_ref[2 * j + side, a]
                faces[side] = term if faces[side] is None else faces[side] + term
        sums.append(faces)
        if j == 0:
            s.push_send[...] = banded(faces[0], s.push.at[0, 0])

            @pl.when(me > 0)
            def _():
                remote(s.push_send, s.placed_in, s.sem_pl.at[0], s.sem_pl.at[1], me - 1).start()

    placed = [
        [None if j + side == 0 else banded(sums[j][side], s.push.at[j, side]) for side in range(2)]
        for j in range(slabs)
    ]

    loads = [modal[j * (inner + 1) + inner] - placed[j][1] for j in range(slabs)]
    for j in range(slabs - 1):
        loads[j] = loads[j] - placed[j + 1][0]
    local = [per_mode(loads[0], s.pts, 0)]
    for j in range(1, slabs):
        load = loads[j] - banded(local[j - 1], s.ets.at[j - 1])
        if j == slabs - 1:

            @pl.when(me == count - 1)
            def _():
                s.placed_in[...] = jnp.zeros_like(s.placed_in)

            @pl.when(me < count - 1)
            def _():
                remote(s.push_send, s.placed_in, s.sem_pl.at[0], s.sem_pl.at[1], me).wait_recv()

            load = load - s.placed_in[...]
        local.append(per_mode(load, s.pts, j))
    offset = per_mode(local[0], s.uts, 0)
    for j in range(1, slabs):
        offset = offset + per_mode(local[j], s.uts, j)
    s.vec_send[...] = jnp.zeros_like(s.vec_send)
    for m in range(mode_dev):
        s.vec_send[m, 0:2, :] = local[-1][2 * m : 2 * m + 2]
        s.vec_send[m, 2:4, :] = offset[2 * m : 2 * m + 2]
    swap = remote(
        s.vec_send.at[pl.ds(half * other, half)], s.pair_vecs.at[core], s.sem_pv.at[0], s.sem_pv.at[1], partner
    )
    swap.start()
    s.pair_vecs[core] = s.vec_send[pl.ds(half * core, half)]
    swap.wait()
    low = lax.broadcasted_iota(jnp.int32, (8, n), 0) < 2
    for i in range(half):
        t0, t1 = s.pair_vecs[0, i], s.pair_vecs[1, i]
        b0 = s.pair_maps[0, i, 1]
        a1, c1 = s.pair_maps[1, i, 0], s.pair_maps[1, i, 2]
        inside = t1 + pltpu.roll(mul(t0, c1), 2, 0)
        s.chip_vecs[i] = jnp.where(low, mul(t0, a1) + t1, t0 + mul(inside, b0))
        owner = half * core + i

        @pl.when(owner != chip)
        def _():
            remote(
                s.chip_vecs.at[i], s.own_vecs.at[chip], s.sem_cv_s.at[i], s.sem_cv_r.at[chip], 2 * owner + core
            ).start()

        @pl.when(owner == chip)
        def _():
            s.own_vecs[chip] = s.chip_vecs[i]

    mine = chip - half * core

    @pl.when(chip // half == core)
    def _():
        for z in range(chips):

            @pl.when(z != chip)
            def _():
                remote(s.chip_vecs.at[0], s.own_vecs.at[z], s.sem_cv_s.at[0], s.sem_cv_r.at[z], me).wait_recv()
                two = pl.ds(0, 2)
                if 0 < z < chips - 1:
                    remote(
                        s.chip_maps.at[0, two], s.own_maps.at[z, two], s.sem_cm_s.at[0, 0], s.sem_cm_r.at[z, 0], me
                    ).wait_recv()
                if z > 0:
                    remote(
                        s.chip_maps.at[0, 2], s.own_maps.at[z, 2], s.sem_cm_s.at[0, 1], s.sem_cm_r.at[z, 1], me
                    ).wait_recv()

        state = jnp.zeros((8, n), F32)
        before = []
        terms = []
        for z in range(chips):
            before.append(state)
            if z > 0:
                terms.append(s.own_vecs[z] + pltpu.roll(mul(state, s.own_maps[z, 2]), 2, 0))
                if z < chips - 1:
                    state = mul(state, s.own_maps[z, 0]) + s.own_vecs[z]
            else:
                terms.append(s.own_vecs[z])
                state = s.own_vecs[z]
        state = jnp.zeros((8, n), F32)
        for z in reversed(range(chips)):
            s.back_send[z] = jnp.where(low, before[z], state)

            @pl.when(z != chip)
            def _():
                remote(s.back_send.at[z], s.back_vecs.at[mine], s.sem_bk_s.at[z], s.sem_bk_r.at[mine], 2 * z + core).start()

            @pl.when(z == chip)
            def _():
                s.back_vecs[mine] = s.back_send[z]

            if z > 0:
                state = terms[z] if z == chips - 1 else mul(state, s.own_maps[z, 1]) + terms[z]

    for i in range(half):

        @pl.when(half * core + i != chip)
        def _():
            remote(s.back_send.at[0], s.back_vecs.at[i], s.sem_bk_s.at[0], s.sem_bk_r.at[i], me).wait_recv()

        t0, t1 = s.pair_vecs[0, i], s.pair_vecs[1, i]
        a0 = s.pair_maps[0, i, 0]
        b1, c1 = s.pair_maps[1, i, 1], s.pair_maps[1, i, 2]
        ends = s.back_vecs[i]
        middle = mul(ends, a0) + t0
        turned = mul(ends, b1) + t1 + pltpu.roll(mul(middle, c1), 2, 0)
        for_zero = jnp.where(low, ends, turned)
        for_one = jnp.where(low, middle, ends)
        s.fin[half * core + i] = jnp.where(core == 0, for_zero, for_one)
        s.fin_send[i] = jnp.where(core == 0, for_one, for_zero)
    give = remote(s.fin_send, s.fin.at[pl.ds(half * core, half)], s.sem_fn.at[0], s.sem_fn.at[1], partner)
    give.start()
    give.wait_send()
    remote(s.fin_send, s.fin.at[pl.ds(half * other, half)], s.sem_fn.at[0], s.sem_fn.at[1], partner).wait_recv()

    start = jnp.concatenate([s.fin[m, 0:2, :] for m in range(mode_dev)], axis=0)
    end = jnp.concatenate([s.fin[m, 2:4, :] for m in range(mode_dev)], axis=0)
    values = [None] * slabs
    for j in reversed(range(slabs)):
        full = local[j] + per_mode(start, s.nts, j)
        values[j] = full - per_mode(end, s.pts, j)
        if j == slabs - 1:
            s.x_send[...] = values[j]

            @pl.when(me < count - 1)
            def _():
                remote(s.x_send, s.x_in, s.sem_x.at[0], s.sem_x.at[1], me + 1).start()

        if j > 0:
            end = banded(values[j], s.es.at[j - 1])

    for j in reversed(range(slabs)):
        if j == 0:

            @pl.when(me == 0)
            def _():
                s.x_in[...] = jnp.zeros_like(s.x_in)

            @pl.when(me > 0)
            def _():
                remote(s.x_send, s.x_in, s.sem_x.at[0], s.sem_x.at[1], me).wait_recv()

            faces = [s.x_in[...], values[0]]
        else:
            faces = [values[j - 1], values[j]]
        lifted = [banded(faces[side], s.lift.at[j, side]) for side in range(2)]
        spread = [
            lifted[0] * couple_ref[2 * j, a] + lifted[1] * couple_ref[2 * j + 1, a] for a in range(inner)
        ]
        left = []
        for b in range(inner):
            total = spread[0] * axial_ref[j * inner, b]
            for a in range(1, inner):
                total = total + spread[a] * axial_ref[j * inner + a, b]
            left.append(spectral[j][b] - total * inverses[j][b])
        turned = []
        for a in range(inner):
            total = left[0] * axial_ref[j * inner + a, 0]
            for b in range(1, inner):
                total = total + left[b] * axial_ref[j * inner + a, b]
            turned.append(total)
        result = mul_split(jnp.concatenate(turned, axis=0), s.rts[j, 0], s.rts[j, 1])
        base = j * (inner + 1) * n
        for a in range(inner):
            out_ref[:, base + a * n : base + (a + 1) * n] = result[a * rows : (a + 1) * rows]
        out_ref[:, base + inner * n : base + (inner + 1) * n] = values[j]

    @pl.when(me > 0)
    def _():
        remote(s.push_send, s.placed_in, s.sem_pl.at[0], s.sem_pl.at[1], me - 1).wait_send()

    @pl.when(me < count - 1)
    def _():
        remote(s.x_send, s.x_in, s.sem_x.at[0], s.sem_x.at[1], me + 1).wait_send()

    for i in range(half):
        send_map(i, False)

        @pl.when(half * core + i != chip)
        def _():
            owner = 2 * (half * core + i) + core
            remote(s.chip_vecs.at[i], s.own_vecs.at[chip], s.sem_cv_s.at[i], s.sem_cv_r.at[chip], owner).wait_send()

    @pl.when(chip // half == core)
    def _():
        for z in range(chips):

            @pl.when(z != chip)
            def _():
                remote(s.back_send.at[z], s.back_vecs.at[mine], s.sem_bk_s.at[z], s.sem_bk_r.at[mine], 2 * z + core).wait_send()


def fourier_table(planes):
    row = np.arange(planes)[:, None]
    angles = (row // 2 * np.arange(planes)[None, :] % planes) * (2.0 * math.pi / planes)
    return (np.where(row % 2 == 0, np.cos(angles), -np.sin(angles)) / math.sqrt(planes)).astype(np.float32)


VMEM = pl.BlockSpec(memory_space=pltpu.VMEM)
SMEM = pl.BlockSpec(memory_space=pltpu.SMEM)
HBM = pl.BlockSpec(memory_space=pltpu.HBM)
LOADED = ("rhs", "table", "panel", "band", "radial", "stiff", "mass")


def body(
    rhs_phys,
    radial_basis,
    axial_basis,
    radial_eig,
    axial_eig,
    face_stiff,
    face_mass,
    axial_coupling,
    face_numbering,
    band_panels,
    inverse_panels,
):
    planes = rhs_phys.shape[0]
    mode_dev, slabs, n = inverse_panels.shape[:3]
    inner = axial_basis.shape[1]
    mode_axis = lax.axis_size("mode")
    chips = lax.axis_size("elem") // 2
    mode_total = mode_dev * mode_axis
    rows = 2 * mode_dev
    half = mode_dev // 2
    parts = half // max(half // 2, 1)
    width = rhs_phys.shape[1]

    table = fourier_table(planes)
    table_high = table.astype(ml_dtypes.bfloat16)
    table = np.stack([table_high, (table - table_high.astype(np.float32)).astype(ml_dtypes.bfloat16)])
    loaded = (rhs_phys, jnp.asarray(table), inverse_panels, band_panels, radial_basis, face_stiff, face_mass)

    def V(*shape, dtype=F32):
        return pltpu.VMEM(shape, dtype)

    def D(*shape):
        return pltpu.SemaphoreType.DMA(shape)

    scratch = {name: V(*array.shape, dtype=array.dtype) for name, array in zip(LOADED, loaded)}
    scratch.update(
        rs=V(slabs, 2, n, n, dtype=BF16),
        rts=V(slabs, 2, n, n, dtype=BF16),
        push=V(slabs, 2, 2, 2 * n, n, dtype=BF16),
        lift=V(slabs, 2, 2, 2 * n, n, dtype=BF16),
        es=V(slabs - 1, 2, 2 * n, n, dtype=BF16),
        ets=V(slabs - 1, 2, 2 * n, n, dtype=BF16),
        maps=V(mode_dev, 3, n, n),
        pts=V(mode_dev, slabs, 2, n, n, dtype=BF16),
        uts=V(mode_dev, slabs, 2, n, n, dtype=BF16),
        nts=V(mode_dev, slabs, 2, n, n, dtype=BF16),
        spec_out=V(mode_axis, rows, width),
        spec_in=V(mode_axis, rows, width),
        placed_in=V(rows, n),
        x_in=V(rows, n),
        x_send=V(rows, n),
        push_send=V(rows, n),
        pair_maps=V(2, half, 3, n, n),
        chip_maps=V(half, 3, n, n),
        own_maps=V(chips, 3, n, n),
        vec_send=V(mode_dev, 8, n),
        pair_vecs=V(2, half, 8, n),
        chip_vecs=V(half, 8, n),
        own_vecs=V(chips, 8, n),
        back_send=V(chips, 8, n),
        back_vecs=V(half, 8, n),
        fin_send=V(half, 8, n),
        fin=V(mode_dev, 8, n),
        sem_in=D(len(LOADED)),
        sem_sp=D(2),
        sem_pm_s=D(parts),
        sem_pm_r=D(parts),
        sem_cm_s=D(half, 2),
        sem_cm_r=D(chips, 2),
        sem_pl=D(2),
        sem_pv=D(2),
        sem_cv_s=D(half),
        sem_cv_r=D(chips),
        sem_bk_s=D(chips),
        sem_bk_r=D(half),
        sem_fn=D(2),
        sem_x=D(2),
    )
    names = [name + "_hbm" for name in LOADED] + ["out"] + list(scratch)
    return pl.pallas_call(
        functools.partial(solve_kernel, names, mode_axis, mode_dev, mode_total, chips),
        out_shape=jax.ShapeDtypeStruct((rows, slabs * (inner + 1) * n), F32),
        in_specs=[SMEM] * 3 + [VMEM] * 2 + [HBM] * len(LOADED),
        out_specs=VMEM,
        scratch_shapes=list(scratch.values()),
        compiler_params=pltpu.CompilerParams(
            collective_id=0, has_side_effects=True, vmem_limit_bytes=56 << 20
        ),
        name="pressure_solve",
    )(
        axial_basis.reshape(slabs * inner, inner),
        axial_coupling.reshape(2 * slabs, inner),
        axial_eig,
        radial_eig,
        face_numbering.reshape(2 * slabs, n),
        *loaded,
    )


def solution(mesh):
    placed = (
        P(None, ("elem", "mode")),
        P("elem", None, None),
        P("elem", None, None),
        P("elem", None),
        P("elem", None),
        P("elem", None, None),
        P("elem", None, None),
        P("elem", None, None),
        P("elem", None, None),
        P(None, "elem", None, None),
        P("mode", "elem", None, None),
    )
    return jax.shard_map(
        body, mesh=mesh, in_specs=placed, out_specs=P("mode", "elem"), check_vma=False
    )
```

time: 86 us -> 63.4 us (0.74)
  starting transfers between devices: 10.6 us -> 0 us
  local copies, waits for them, and re-layouts: 14.2 us -> 7.23 us
  matrix products: 2.51 us -> 0 us
  Pallas kernels: 58.1 us -> 55.9 us
    all_to_all x1 -> x0, starting transfers between devices: 10.6 us -> none  [body(): lax.all_to_all(spectrum.reshape(mode_axis, rows, -1), 'mode', split_axis=...]
    unnamed x45 -> x2, local copies, waits for them, and re-layouts: 13.6 us -> 3.37 us
    dot_general x1 -> x0, matrix products: 2.51 us -> none  [body(): jnp.dot(jnp.asarray(fourier_table(planes)), rhs_phys, precision=HIGH, pre...]
    pallas_call x3 -> x1, Pallas kernels: 58.1 us -> 55.9 us  [body(): pl.pallas_call(functools.partial(solve_kernel, names, mode_axis, mode_dev...]
    reshape x1, local copies, waits for them, and re-layouts: 0.01 us -> 1.31 us  [body(): axial_basis.reshape(slabs * inner, inner)]
    reshape x1, local copies, waits for them, and re-layouts: 0.01 us -> 1.27 us  [body(): axial_coupling.reshape(2 * slabs, inner)]
  transfers between devices with their start and end apart: 1 -> 0, of which waited for: 0 -> 0; matrix products, arithmetic and copies ran while one was open for 1% -> 0% of each run, Pallas kernels for 14% -> 0%
where the time goes in v2:
time: 63.4 us; the launch traced here: 63.1 us
  Pallas kernels  55.9 us (88%)
  local copies, waits for them, and re-layouts  7.23 us (11%)
    pallas_call x1, Pallas kernels, body(): pl.pallas_call(functools.partial(solve_kernel, names, mode_axis, mode_dev...  55.9 us
    unnamed x2, local copies, waits for them, and re-layouts  3.37 us
    reshape x1, local copies, waits for them, and re-layouts, body(): axial_basis.reshape(slabs * inner, inner)  1.31 us
    reshape x1, local copies, waits for them, and re-layouts, body(): face_numbering.reshape(2 * slabs, n)  1.28 us
    reshape x1, local copies, waits for them, and re-layouts, body(): axial_coupling.reshape(2 * slabs, inner)  1.27 us

profile of v2, /device:TPU:1, one launch (start us, length us, event | category | flops | bytes accessed | tf_op | source)
XLA Modules:
  0.0 63.1 jit_solution(16747429048087820500)
XLA Ops:
  0.0 1.3 %reshape.10.couple_ref = f32[6,7]{1,0:T(8,128)} reshape(f32[3,2,7]{2,1,0:T(2,128)} %param.19) | data formatting | bytes 336 | tf_op jit(solution)/shard_map/reshape | solution.py:636
  1.3 1.3 %reshape.11.number_ref = s32[6,128]{1,0:T(8,128)} reshape(s32[3,2,128]{2,1,0:T(2,128)} %param.20) | data formatting | bytes 6144 | tf_op jit(solution)/shard_map/reshape | solution.py:639
  2.6 1.3 %reshape.12.axial_ref = f32[21,7]{1,0:T(8,128)} reshape(f32[3,7,7]{2,1,0:T(8,128)} %param.14) | data formatting | bytes 1176 | tf_op jit(solution)/shard_map/reshape | solution.py:635
  3.9 1.8 %copy.16.refs_0_ = f32[512,96]{1,0:T(8,128)} copy(f32[512,96]{0,1:T(8,128)} %param.12) | data formatting | bytes 393216 | tf_op args[0]
  5.6 55.9 %pressure_solve.1 = f32[16,3072]{1,0:T(8,128)} custom-call(f32[21,7]{1,0:T(8,128)} %reshape.12.axial_ref, f32[6,7]{1,0:T(8,128)} %reshape.10.couple_ref, f32[3,7]{1,0:T(4,128)} %axial_eig_ref.1, f32[3,128]{1,0:T(4,128)} %radial_eig_ref.1, s32[6,128]{1,0:T(8,128)} %reshape.11.number_ref, f32[512,96]{1,0:T(8,128)} %copy.16.refs_0_, ...), custom_call_target="tpu_custom_call" | custom-call | tf_op jit(solution)/shard_map/pressure_solve/pallas_call | solution.py:624
  61.5 1.6 %copy.19 = f32[16,3072]{1,0:T(8,128)} copy(f32[16,3072]{1,0:T(8,128)} %pressure_solve.1) | data formatting | bytes 393216

commit v3 on v2

--- a/solution.py
+++ b/solution.py
@@ -13,7 +13,6 @@
 
 F32 = jnp.float32
 BF16 = jnp.bfloat16
-HIGH = lax.Precision.HIGH
 
 
 def split(x):
@@ -23,6 +22,10 @@
 
 def bdot(a, b):
     return jnp.dot(a, b, preferred_element_type=F32)
+
+
+def bdot_turned(a, b):
+    return lax.dot_general(a, b, (((1,), (1,)), ((), ())), preferred_element_type=F32)
 
 
 def mul_split(v, hi, lo):
@@ -56,7 +59,7 @@
             turned.append(split(mul(face[j].T, basis)))
     for j in range(slabs):
         for side in range(2):
-            numbers = number_ref[2 * j + side : 2 * j + side + 1, :]
+            numbers = number_ref[j, side : side + 1, :]
             hot = (lax.broadcasted_iota(jnp.int32, (n, n), 0) == numbers).astype(F32).astype(BF16)
             for part in range(2):
                 th, tl = turned[2 * j + part]
@@ -78,7 +81,7 @@
     return bdot(a[0], b[0]) + (bdot(a[1], b[0]) + bdot(a[0], b[1]))
 
 
-def mode_maps(s, modes, first, mode_total):
+def mode_maps(s, core, modes, first, mode_total):
     slabs = s.panel.shape[1]
     count = len(modes)
     turned = [[s.band[p, j].T for p in range(2)] for j in range(slabs)]
@@ -110,14 +113,14 @@
             backed = -times(pts[i][j], back[i])
             back[i] = split(backed)
             if j == slabs - 1:
-                s.maps[m, 0] = full
-                s.maps[m, 1] = backed
+                s.both[core, m, 0] = full
+                s.both[core, m, 1] = backed
     for j in range(slabs):
         for i in range(count):
             term = times(*nears[i][j])
             cross[i] = term if cross[i] is None else cross[i] + term
     for i, m in enumerate(modes):
-        s.maps[m, 2] = cross[i]
+        s.both[core, m, 2] = cross[i]
 
 
 def solve_kernel(
@@ -138,14 +141,13 @@
     slabs, n = s.rs.shape[0], s.rs.shape[-1]
     rows = 2 * mode_dev
     half = mode_dev // 2
-    inner = axial_ref.shape[0] // slabs
+    inner = axial_ref.shape[1]
     me = lax.axis_index("elem")
     count = 2 * chips
     core = lax.rem(me, 2)
     chip = me // 2
     other = 1 - core
     partner = 2 * chip + other
-    across = lax.rem(me + count - 1 + 2 * core, count)
 
     fetch = []
     for at, name in enumerate(LOADED):
@@ -157,10 +159,8 @@
     line = lax.axis_index("mode")
     for k in range(1, mode_axis):
         pl.semaphore_signal(barrier, 1, device_id={"mode": lax.rem(line + k, mode_axis)})
-    for k in range(1, chips):
-        pl.semaphore_signal(barrier, 1, device_id={"elem": 2 * lax.rem(chip + k, chips) + core})
-    pl.semaphore_signal(barrier, 1, device_id={"elem": partner})
-    pl.semaphore_signal(barrier, 1, device_id={"elem": across})
+    for k in range(1, count):
+        pl.semaphore_signal(barrier, 1, device_id={"elem": lax.rem(me + k, count)})
 
     def remote(src, dst, send, recv, device):
         return pltpu.make_async_remote_copy(
@@ -191,15 +191,26 @@
 
     for copy in fetch[:2]:
         copy.wait()
-    rhs = split(s.rhs[...])
-    spectrum = bdot(s.table[0], rhs[0]) + (bdot(s.table[1], rhs[0]) + bdot(s.table[0], rhs[1]))
-    s.spec_out[...] = spectrum.reshape(s.spec_out.shape)
-    for copy in fetch[2:4]:
-        copy.wait()
     first = line * mode_dev
     quarter = max(half // 2, 1)
     parts = [range(at, min(at + quarter, half)) for at in range(0, half, quarter)]
-    pl.semaphore_wait(barrier, mode_axis + chips)
+    shares = [[], []]
+    for at, part in enumerate(parts):
+        modes = [half * other + i for i in part] + [half * core + i for i in part]
+        mode_maps(s, core, modes, first, mode_total)
+        if at == 0:
+            pl.semaphore_wait(barrier, mode_axis - 1 + count - 1)
+        for whose, taken in ((other, 0), (core, 1)):
+            block = s.both.at[core, pl.ds(half * whose + part[0], len(part))]
+            share = remote(block, block, s.sem_pm_s.at[taken, at], s.sem_pm_r.at[taken, at], partner)
+            share.start()
+            shares[taken].append(share)
+
+    for copy in fetch[2:4]:
+        copy.wait()
+    rhs = split(s.rhs[...])
+    spectrum = bdot_turned(s.table[0], rhs[0]) + (bdot_turned(s.table[1], rhs[0]) + bdot_turned(s.table[0], rhs[1]))
+    s.spec_out[...] = spectrum.reshape(s.spec_out.shape)
 
     def spread_out(k, carry):
         to = lax.rem(line + k, mode_axis)
@@ -216,21 +227,6 @@
     lax.fori_loop(1, mode_axis, spread_out, 0)
     s.spec_in[line] = s.spec_out[line]
 
-    shares = []
-    for at, part in enumerate(parts):
-        modes = [half * other + i for i in part] + [half * core + i for i in part]
-        mode_maps(s, modes, first, mode_total)
-        share = remote(
-            s.maps.at[pl.ds(half * other + part[0], len(part))],
-            s.pair_maps.at[core, pl.ds(part[0], len(part))],
-            s.sem_pm_s.at[at],
-            s.sem_pm_r.at[at],
-            partner,
-        )
-        share.start()
-        shares.append(share)
-
-    s.pair_maps[core] = s.maps[pl.ds(half * core, half)]
 
     def send_map(i, start):
         owner = half * core + i
@@ -255,9 +251,9 @@
         def _():
             cross.start() if start else cross.wait_send()
 
-    for part, share in zip(parts, shares):
+    for part, share in zip(parts, shares[0]):
         share.wait()
-        pair = [[[split(s.pair_maps[c, i, k]) for k in range(3)] for c in range(2)] for i in part]
+        pair = [[[split(s.both[c, half * core + i, k]) for k in range(3)] for c in range(2)] for i in part]
         ahead = [times(one[0][0], one[1][0]) for one in pair]
         back = [times(one[1][1], one[0][1]) for one in pair]
         cross = [split(times(one[0][0], one[1][2])) for one in pair]
@@ -265,7 +261,7 @@
         for at, i in enumerate(part):
             s.chip_maps[i, 0] = ahead[at]
             s.chip_maps[i, 1] = back[at]
-            s.chip_maps[i, 2] = s.pair_maps[0, i, 2] + cross[at]
+            s.chip_maps[i, 2] = s.both[0, half * core + i, 2] + cross[at]
         for i in part:
             send_map(i, True)
 
@@ -306,9 +302,9 @@
         values = []
         scales = []
         for b in range(inner):
-            total = x[:rows] * axial_ref[j * inner, b]
+            total = x[:rows] * axial_ref[j, 0, b]
             for a in range(1, inner):
-                total = total + x[a * rows : (a + 1) * rows] * axial_ref[j * inner + a, b]
+                total = total + x[a * rows : (a + 1) * rows] * axial_ref[j, a, b]
             scale = 1.0 / (axial_eig_ref[j, b] + radial_eig_ref[j : j + 1, :] + lam)
             scales.append(scale)
             values.append(total * scale)
@@ -316,11 +312,11 @@
         inverses.append(scales)
         faces = [None, None]
         for a in range(inner):
-            total = values[0] * axial_ref[j * inner + a, 0]
+            total = values[0] * axial_ref[j, a, 0]
             for b in range(1, inner):
-                total = total + values[b] * axial_ref[j * inner + a, b]
+                total = total + values[b] * axial_ref[j, a, b]
             for side in range(2):
-                term = total * couple_ref[2 * j + side, a]
+                term = total * couple_ref[j, side, a]
                 faces[side] = term if faces[side] is None else faces[side] + term
         sums.append(faces)
         if j == 0:
@@ -360,40 +356,59 @@
     for m in range(mode_dev):
         s.vec_send[m, 0:2, :] = local[-1][2 * m : 2 * m + 2]
         s.vec_send[m, 2:4, :] = offset[2 * m : 2 * m + 2]
-    swap = remote(
-        s.vec_send.at[pl.ds(half * other, half)], s.pair_vecs.at[core], s.sem_pv.at[0], s.sem_pv.at[1], partner
-    )
+    swap = remote(s.vec_send, s.mate_vecs, s.sem_pv.at[0], s.sem_pv.at[1], partner)
     swap.start()
-    s.pair_vecs[core] = s.vec_send[pl.ds(half * core, half)]
-    swap.wait()
+    for share in shares[1]:
+        share.wait()
     low = lax.broadcasted_iota(jnp.int32, (8, n), 0) < 2
-    for i in range(half):
-        t0, t1 = s.pair_vecs[0, i], s.pair_vecs[1, i]
-        b0 = s.pair_maps[0, i, 1]
-        a1, c1 = s.pair_maps[1, i, 0], s.pair_maps[1, i, 2]
-        inside = t1 + pltpu.roll(mul(t0, c1), 2, 0)
-        s.chip_vecs[i] = jnp.where(low, mul(t0, a1) + t1, t0 + mul(inside, b0))
-        owner = half * core + i
-
-        @pl.when(owner != chip)
+
+    @pl.when(core == 0)
+    def _():
+        for m in range(mode_dev):
+            tile = s.vec_send[m]
+            turned = mul(mul(tile, s.both[1, m, 2]), s.both[0, m, 1])
+            s.chip_vecs[m] = jnp.where(low, mul(tile, s.both[1, m, 0]), tile + pltpu.roll(turned, 2, 0))
+
+    @pl.when(core == 1)
+    def _():
+        for m in range(mode_dev):
+            tile = s.vec_send[m]
+            s.chip_vecs[m] = jnp.where(low, tile, mul(tile, s.both[0, m, 1]))
+
+    def vector_copy(m):
+        return remote(
+            s.chip_vecs.at[m],
+            s.own_vecs.at[core, chip],
+            s.sem_cv_s.at[m],
+            s.sem_cv_r.at[core, chip],
+            2 * m + m // half,
+        )
+
+    for m in range(mode_dev):
+
+        @pl.when(me != 2 * m + m // half)
         def _():
-            remote(
-                s.chip_vecs.at[i], s.own_vecs.at[chip], s.sem_cv_s.at[i], s.sem_cv_r.at[chip], 2 * owner + core
-            ).start()
-
-        @pl.when(owner == chip)
+            vector_copy(m).start()
+
+        @pl.when(me == 2 * m + m // half)
         def _():
-            s.own_vecs[chip] = s.chip_vecs[i]
-
-    mine = chip - half * core
-
-    @pl.when(chip // half == core)
+            s.own_vecs[core, chip] = s.chip_vecs[m]
+
+    owner = chip // half == core
+
+    @pl.when(owner)
     def _():
         for z in range(chips):
+            for c in range(2):
+
+                @pl.when(2 * z + c != me)
+                def _():
+                    remote(
+                        s.chip_vecs.at[0], s.own_vecs.at[c, z], s.sem_cv_s.at[0], s.sem_cv_r.at[c, z], me
+                    ).wait_recv()
 
             @pl.when(z != chip)
             def _():
-                remote(s.chip_vecs.at[0], s.own_vecs.at[z], s.sem_cv_s.at[0], s.sem_cv_r.at[z], me).wait_recv()
                 two = pl.ds(0, 2)
                 if 0 < z < chips - 1:
                     remote(
@@ -404,53 +419,61 @@
                         s.chip_maps.at[0, 2], s.own_maps.at[z, 2], s.sem_cm_s.at[0, 1], s.sem_cm_r.at[z, 1], me
                     ).wait_recv()
 
+        vecs = [s.own_vecs[0, z] + s.own_vecs[1, z] for z in range(chips)]
         state = jnp.zeros((8, n), F32)
         before = []
         terms = []
         for z in range(chips):
             before.append(state)
             if z > 0:
-                terms.append(s.own_vecs[z] + pltpu.roll(mul(state, s.own_maps[z, 2]), 2, 0))
+                terms.append(vecs[z] + pltpu.roll(mul(state, s.own_maps[z, 2]), 2, 0))
                 if z < chips - 1:
-                    state = mul(state, s.own_maps[z, 0]) + s.own_vecs[z]
+                    state = mul(state, s.own_maps[z, 0]) + vecs[z]
             else:
-                terms.append(s.own_vecs[z])
-                state = s.own_vecs[z]
+                terms.append(vecs[z])
+                state = vecs[z]
         state = jnp.zeros((8, n), F32)
         for z in reversed(range(chips)):
             s.back_send[z] = jnp.where(low, before[z], state)
-
-            @pl.when(z != chip)
-            def _():
-                remote(s.back_send.at[z], s.back_vecs.at[mine], s.sem_bk_s.at[z], s.sem_bk_r.at[mine], 2 * z + core).start()
+            for c in range(2):
+
+                @pl.when(2 * z + c != me)
+                def _():
+                    remote(
+                        s.back_send.at[z],
+                        s.back_vecs.at[chip],
+                        s.sem_bk_s.at[z, c],
+                        s.sem_bk_r.at[chip],
+                        2 * z + c,
+                    ).start()
 
             @pl.when(z == chip)
             def _():
-                s.back_vecs[mine] = s.back_send[z]
+                s.back_vecs[chip] = s.back_send[z]
 
             if z > 0:
                 state = terms[z] if z == chips - 1 else mul(state, s.own_maps[z, 1]) + terms[z]
 
-    for i in range(half):
-
-        @pl.when(half * core + i != chip)
+    swap.wait()
+    for m in range(mode_dev):
+
+        @pl.when(me != 2 * m + m // half)
         def _():
-            remote(s.back_send.at[0], s.back_vecs.at[i], s.sem_bk_s.at[0], s.sem_bk_r.at[i], me).wait_recv()
-
-        t0, t1 = s.pair_vecs[0, i], s.pair_vecs[1, i]
-        a0 = s.pair_maps[0, i, 0]
-        b1, c1 = s.pair_maps[1, i, 1], s.pair_maps[1, i, 2]
-        ends = s.back_vecs[i]
-        middle = mul(ends, a0) + t0
-        turned = mul(ends, b1) + t1 + pltpu.roll(mul(middle, c1), 2, 0)
-        for_zero = jnp.where(low, ends, turned)
-        for_one = jnp.where(low, middle, ends)
-        s.fin[half * core + i] = jnp.where(core == 0, for_zero, for_one)
-        s.fin_send[i] = jnp.where(core == 0, for_one, for_zero)
-    give = remote(s.fin_send, s.fin.at[pl.ds(half * core, half)], s.sem_fn.at[0], s.sem_fn.at[1], partner)
-    give.start()
-    give.wait_send()
-    remote(s.fin_send, s.fin.at[pl.ds(half * other, half)], s.sem_fn.at[0], s.sem_fn.at[1], partner).wait_recv()
+            remote(s.back_send.at[0], s.back_vecs.at[m], s.sem_bk_s.at[0, 0], s.sem_bk_r.at[m], me).wait_recv()
+
+    @pl.when(core == 0)
+    def _():
+        for m in range(mode_dev):
+            ends = s.back_vecs[m]
+            middle = mul(ends, s.both[0, m, 0]) + s.vec_send[m]
+            turned = mul(ends, s.both[1, m, 1]) + s.mate_vecs[m]
+            s.fin[m] = jnp.where(low, ends, turned + pltpu.roll(mul(middle, s.both[1, m, 2]), 2, 0))
+
+    @pl.when(core == 1)
+    def _():
+        for m in range(mode_dev):
+            ends = s.back_vecs[m]
+            s.fin[m] = jnp.where(low, mul(ends, s.both[0, m, 0]) + s.mate_vecs[m], ends)
 
     start = jnp.concatenate([s.fin[m, 0:2, :] for m in range(mode_dev)], axis=0)
     end = jnp.concatenate([s.fin[m, 2:4, :] for m in range(mode_dev)], axis=0)
@@ -484,19 +507,19 @@
             faces = [values[j - 1], values[j]]
         lifted = [banded(faces[side], s.lift.at[j, side]) for side in range(2)]
         spread = [
-            lifted[0] * couple_ref[2 * j, a] + lifted[1] * couple_ref[2 * j + 1, a] for a in range(inner)
+            lifted[0] * couple_ref[j, 0, a] + lifted[1] * couple_ref[j, 1, a] for a in range(inner)
         ]
         left = []
         for b in range(inner):
-            total = spread[0] * axial_ref[j * inner, b]
+            total = spread[0] * axial_ref[j, 0, b]
             for a in range(1, inner):
-                total = total + spread[a] * axial_ref[j * inner + a, b]
+                total = total + spread[a] * axial_ref[j, a, b]
             left.append(spectral[j][b] - total * inverses[j][b])
         turned = []
         for a in range(inner):
-            total = left[0] * axial_ref[j * inner + a, 0]
+            total = left[0] * axial_ref[j, a, 0]
             for b in range(1, inner):
-                total = total + left[b] * axial_ref[j * inner + a, b]
+                total = total + left[b] * axial_ref[j, a, b]
             turned.append(total)
         result = mul_split(jnp.concatenate(turned, axis=0), s.rts[j, 0], s.rts[j, 1])
         base = j * (inner + 1) * n
@@ -514,19 +537,26 @@
 
     for i in range(half):
         send_map(i, False)
-
-        @pl.when(half * core + i != chip)
+    for m in range(mode_dev):
+
+        @pl.when(me != 2 * m + m // half)
         def _():
-            owner = 2 * (half * core + i) + core
-            remote(s.chip_vecs.at[i], s.own_vecs.at[chip], s.sem_cv_s.at[i], s.sem_cv_r.at[chip], owner).wait_send()
-
-    @pl.when(chip // half == core)
+            vector_copy(m).wait_send()
+
+    @pl.when(owner)
     def _():
         for z in range(chips):
-
-            @pl.when(z != chip)
-            def _():
-                remote(s.back_send.at[z], s.back_vecs.at[mine], s.sem_bk_s.at[z], s.sem_bk_r.at[mine], 2 * z + core).wait_send()
+            for c in range(2):
+
+                @pl.when(2 * z + c != me)
+                def _():
+                    remote(
+                        s.back_send.at[z],
+                        s.back_vecs.at[chip],
+                        s.sem_bk_s.at[z, c],
+                        s.sem_bk_r.at[chip],
+                        2 * z + c,
+                    ).wait_send()
 
 
 def fourier_table(planes):
@@ -538,7 +568,7 @@
 VMEM = pl.BlockSpec(memory_space=pltpu.VMEM)
 SMEM = pl.BlockSpec(memory_space=pltpu.SMEM)
 HBM = pl.BlockSpec(memory_space=pltpu.HBM)
-LOADED = ("rhs", "table", "panel", "band", "radial", "stiff", "mass")
+LOADED = ("panel", "band", "rhs", "table", "radial", "stiff", "mass")
 
 
 def body(
@@ -568,7 +598,7 @@
     table = fourier_table(planes)
     table_high = table.astype(ml_dtypes.bfloat16)
     table = np.stack([table_high, (table - table_high.astype(np.float32)).astype(ml_dtypes.bfloat16)])
-    loaded = (rhs_phys, jnp.asarray(table), inverse_panels, band_panels, radial_basis, face_stiff, face_mass)
+    loaded = (inverse_panels, band_panels, rhs_phys.T, jnp.asarray(table), radial_basis, face_stiff, face_mass)
 
     def V(*shape, dtype=F32):
         return pltpu.VMEM(shape, dtype)
@@ -584,7 +614,6 @@
         lift=V(slabs, 2, 2, 2 * n, n, dtype=BF16),
         es=V(slabs - 1, 2, 2 * n, n, dtype=BF16),
         ets=V(slabs - 1, 2, 2 * n, n, dtype=BF16),
-        maps=V(mode_dev, 3, n, n),
         pts=V(mode_dev, slabs, 2, n, n, dtype=BF16),
         uts=V(mode_dev, slabs, 2, n, n, dtype=BF16),
         nts=V(mode_dev, slabs, 2, n, n, dtype=BF16),
@@ -594,30 +623,28 @@
         x_in=V(rows, n),
         x_send=V(rows, n),
         push_send=V(rows, n),
-        pair_maps=V(2, half, 3, n, n),
+        both=V(2, mode_dev, 3, n, n),
         chip_maps=V(half, 3, n, n),
         own_maps=V(chips, 3, n, n),
         vec_send=V(mode_dev, 8, n),
-        pair_vecs=V(2, half, 8, n),
-        chip_vecs=V(half, 8, n),
-        own_vecs=V(chips, 8, n),
+        mate_vecs=V(mode_dev, 8, n),
+        chip_vecs=V(mode_dev, 8, n),
+        own_vecs=V(2, chips, 8, n),
         back_send=V(chips, 8, n),
-        back_vecs=V(half, 8, n),
-        fin_send=V(half, 8, n),
+        back_vecs=V(mode_dev, 8, n),
         fin=V(mode_dev, 8, n),
         sem_in=D(len(LOADED)),
         sem_sp=D(2),
-        sem_pm_s=D(parts),
-        sem_pm_r=D(parts),
+        sem_pm_s=D(2, parts),
+        sem_pm_r=D(2, parts),
         sem_cm_s=D(half, 2),
         sem_cm_r=D(chips, 2),
         sem_pl=D(2),
         sem_pv=D(2),
-        sem_cv_s=D(half),
-        sem_cv_r=D(chips),
-        sem_bk_s=D(chips),
-        sem_bk_r=D(half),
-        sem_fn=D(2),
+        sem_cv_s=D(mode_dev),
+        sem_cv_r=D(2, chips),
+        sem_bk_s=D(chips, 2),
+        sem_bk_r=D(mode_dev),
         sem_x=D(2),
     )
     names = [name + "_hbm" for name in LOADED] + ["out"] + list(scratch)
@@ -632,11 +659,11 @@
         ),
         name="pressure_solve",
     )(
-        axial_basis.reshape(slabs * inner, inner),
-        axial_coupling.reshape(2 * slabs, inner),
+        axial_basis,
+        axial_coupling,
         axial_eig,
         radial_eig,
-        face_numbering.reshape(2 * slabs, n),
+        face_numbering,
         *loaded,
     )
 

time: 63.4 us -> 56.1 us (0.88)
  local copies, waits for them, and re-layouts: 7.23 us -> 1.62 us
  Pallas kernels: 55.9 us -> 54.2 us
    reshape x3 -> x0, local copies, waits for them, and re-layouts: 3.86 us -> none  [the longest x1 1.31 us: body(): axial_basis.reshape(slabs * inner, inner)]
    unnamed x2 -> x1, local copies, waits for them, and re-layouts: 3.37 us -> 1.62 us
    pallas_call x1, Pallas kernels: 55.9 us -> 54.2 us  [body(): pl.pallas_call(functools.partial(solve_kernel, names, mode_axis, mode_dev...]
where the time goes in v3:
time: 56.1 us; the launch traced here: 55.9 us
  Pallas kernels  54.2 us (97%)
  local copies, waits for them, and re-layouts  1.62 us (3%)
    pallas_call x1, Pallas kernels, body(): pl.pallas_call(functools.partial(solve_kernel, names, mode_axis, mode_dev...  54.2 us
    unnamed x1, local copies, waits for them, and re-layouts  1.62 us

profile of v3, /device:TPU:1, one launch (start us, length us, event | category | flops | bytes accessed | tf_op | source)
XLA Modules:
  0.0 55.9 jit_solution(1328614733051020883)
XLA Ops:
  0.0 54.2 %pressure_solve.1 = f32[16,3072]{1,0:T(8,128)} custom-call(f32[3,7,7]{2,1,0:T(8,128)} %axial_ref.1, f32[3,2,7]{2,1,0:T(2,128)} %couple_ref.1, f32[3,7]{1,0:T(4,128)} %axial_eig_ref.1, f32[3,128]{1,0:T(4,128)} %radial_eig_ref.1, s32[3,2,128]{2,1,0:T(2,128)} %number_ref.1, f32[8,3,128,128]{3,2,1,0:T(8,128)} %refs_0_.1, f32[2,3,128,128]{3,2,1,0:T(8,128)} %refs_1_.1, ...), custom_call_target="tpu_custom_call" | custom-call | tf_op jit(solution)/shard_map/pressure_solve/pallas_call | solution.py:651
  54.3 1.6 %copy.14 = f32[16,3072]{1,0:T(8,128)} copy(f32[16,3072]{1,0:T(8,128)} %pressure_solve.1) | data formatting | bytes 393216

commit v4 on v3

--- a/solution.py
+++ b/solution.py
@@ -123,6 +123,51 @@
         s.both[core, m, 2] = cross[i]
 
 
+def last_maps(s, core, modes, first, mode_total):
+    slabs, n = s.panel.shape[1], s.panel.shape[2]
+    where = range(len(modes))
+    lams = [wave_square(first + m, mode_total) for m in modes]
+    bands = [[split(s.band[0, j] + lam * s.band[1, j]) for j in range(1, slabs)] for lam in lams]
+    turns = [[times(bands[i][j], (s.pts[m, j, 0], s.pts[m, j, 1])) for j in range(slabs - 1)] for i, m in enumerate(modes)]
+    turns = [[split(x) for x in row] for row in turns]
+    near = [[None] * slabs for _ in modes]
+    far = [[None] * slabs for _ in modes]
+    for i, m in enumerate(modes):
+        last = slabs - 1
+        near[i][last] = (s.nts[m, last, 0], s.nts[m, last, 1])
+        far[i][last] = (-s.pts[m, last, 0], -s.pts[m, last, 1])
+    for j in reversed(range(slabs - 1)):
+        for i, m in enumerate(modes):
+            here = s.nts[m, j, 0].astype(F32) + s.nts[m, j, 1].astype(F32)
+            near[i][j] = split(here - times(near[i][j + 1], turns[i][j]))
+            far[i][j] = split(-times(far[i][j + 1], turns[i][j]))
+
+    @pl.when(core == 0)
+    def _():
+        outer = [split(s.both[1, m, 1]) for m in modes]
+        cross = [split(mul(s.both[0, m, 0], s.both[1, m, 2])) for m in modes]
+        for j in range(slabs):
+            for i, m in enumerate(modes):
+                whole = near[i][j][0].astype(F32) + near[i][j][1].astype(F32)
+                starts = split(whole + times(cross[i], far[i][j]))
+                ends = split(times(outer[i], far[i][j]))
+                for part in range(2):
+                    s.last[m, j, part, 0:n] = starts[part]
+                    s.last[m, j, part, n : 2 * n] = ends[part]
+                    s.extra[m, j, part] = far[i][j][part]
+
+    @pl.when(core == 1)
+    def _():
+        inner = [split(s.both[0, m, 0]) for m in modes]
+        for j in range(slabs):
+            for i, m in enumerate(modes):
+                starts = split(times(inner[i], near[i][j]))
+                for part in range(2):
+                    s.last[m, j, part, 0:n] = starts[part]
+                    s.last[m, j, part, n : 2 * n] = far[i][j][part]
+                    s.extra[m, j, part] = near[i][j][part]
+
+
 def solve_kernel(
     names,
     mode_axis,
@@ -149,11 +194,20 @@
     other = 1 - core
     partner = 2 * chip + other
 
-    fetch = []
-    for at, name in enumerate(LOADED):
+    parts = [[lax.rem(chip + k, half)] for k in range(half)]
+    fetch = {}
+    for at, name in enumerate(LOADED[1:]):
         copy = pltpu.make_async_copy(getattr(s, name + "_hbm"), getattr(s, name), s.sem_in.at[at])
         copy.start()
-        fetch.append(copy)
+        fetch[name] = copy
+        if at == 0:
+            panels = []
+            for k, part in enumerate(parts):
+                for j, whose in enumerate((other, core)):
+                    block = pl.ds(half * whose + part[0], len(part))
+                    copy = pltpu.make_async_copy(s.panel_hbm.at[block], s.panel.at[block], s.sem_pa.at[k, j])
+                    copy.start()
+                    panels.append(copy)
 
     barrier = pltpu.get_barrier_semaphore()
     line = lax.axis_index("mode")
@@ -176,7 +230,7 @@
     def per_mode(v, ref, *at):
         vh, vl = split(v)
         both = jnp.concatenate([vh, vl], axis=0)
-        sides = lax.broadcasted_iota(jnp.int32, (2 * rows, n), 0)
+        sides = lax.broadcasted_iota(jnp.int32, both.shape, 0)
         sides = jnp.where(sides < rows, sides, sides - rows) // 2
         zero = jnp.zeros_like(both)
         total = None
@@ -189,14 +243,49 @@
             low = term_low if low is None else low + term_low
         return total[:rows] + (total[rows:] + low)
 
-    for copy in fetch[:2]:
-        copy.wait()
+    def send_map(i, k, start):
+        owner = half * core + i
+        away = jnp.logical_and(owner != chip, chip > 0)
+        if k < 2:
+            away = jnp.logical_and(away, chip < chips - 1)
+
+        @pl.when(away)
+        def _():
+            copy = remote(
+                s.chip_maps.at[i, k],
+                s.own_maps.at[chip, k],
+                s.sem_cm_s.at[i, k],
+                s.sem_cm_r.at[chip, k],
+                2 * owner + core,
+            )
+            copy.start() if start else copy.wait_send()
+
+    def pairing(part, share):
+        share.wait()
+        pair = [[[split(s.both[c, half * core + i, k]) for k in range(3)] for c in range(2)] for i in part]
+        ahead = [times(one[0][0], one[1][0]) for one in pair]
+        back = [times(one[1][1], one[0][1]) for one in pair]
+        cross = [split(times(one[0][0], one[1][2])) for one in pair]
+        cross = [times(x, one[0][1]) for x, one in zip(cross, pair)]
+        for at, i in enumerate(part):
+            s.chip_maps[i, 0] = ahead[at]
+            s.chip_maps[i, 1] = back[at]
+            s.chip_maps[i, 2] = s.both[0, half * core + i, 2] + cross[at]
+        for i in part:
+            for k in (0, 2, 1):
+                send_map(i, k, True)
+
+            @pl.when(half * core + i == chip)
+            def _():
+                s.own_maps[chip] = s.chip_maps[i]
+
+    fetch["band"].wait()
     first = line * mode_dev
-    quarter = max(half // 2, 1)
-    parts = [range(at, min(at + quarter, half)) for at in range(0, half, quarter)]
     shares = [[], []]
     for at, part in enumerate(parts):
         modes = [half * other + i for i in part] + [half * core + i for i in part]
+        for copy in panels[2 * at : 2 * at + 2]:
+            copy.wait()
         mode_maps(s, core, modes, first, mode_total)
         if at == 0:
             pl.semaphore_wait(barrier, mode_axis - 1 + count - 1)
@@ -205,9 +294,11 @@
             share = remote(block, block, s.sem_pm_s.at[taken, at], s.sem_pm_r.at[taken, at], partner)
             share.start()
             shares[taken].append(share)
-
-    for copy in fetch[2:4]:
-        copy.wait()
+        if at > 0:
+            pairing(parts[at - 1], shares[0][at - 1])
+
+    fetch["rhs"].wait()
+    fetch["table"].wait()
     rhs = split(s.rhs[...])
     spectrum = bdot_turned(s.table[0], rhs[0]) + (bdot_turned(s.table[1], rhs[0]) + bdot_turned(s.table[0], rhs[1]))
     s.spec_out[...] = spectrum.reshape(s.spec_out.shape)
@@ -227,51 +318,15 @@
     lax.fori_loop(1, mode_axis, spread_out, 0)
     s.spec_in[line] = s.spec_out[line]
 
-
-    def send_map(i, start):
-        owner = half * core + i
-        away = jnp.logical_and(owner != chip, chip > 0)
-        to = 2 * owner + core
-        ends = remote(
-            s.chip_maps.at[i, pl.ds(0, 2)],
-            s.own_maps.at[chip, pl.ds(0, 2)],
-            s.sem_cm_s.at[i, 0],
-            s.sem_cm_r.at[chip, 0],
-            to,
-        )
-        cross = remote(
-            s.chip_maps.at[i, 2], s.own_maps.at[chip, 2], s.sem_cm_s.at[i, 1], s.sem_cm_r.at[chip, 1], to
-        )
-
-        @pl.when(jnp.logical_and(away, chip < chips - 1))
-        def _():
-            ends.start() if start else ends.wait_send()
-
-        @pl.when(away)
-        def _():
-            cross.start() if start else cross.wait_send()
-
-    for part, share in zip(parts, shares[0]):
+    pairing(parts[-1], shares[0][-1])
+    for name in ("radial", "stiff", "mass"):
+        fetch[name].wait()
+    slab_matrices(s, number_ref)
+
+    for share in shares[1]:
         share.wait()
-        pair = [[[split(s.both[c, half * core + i, k]) for k in range(3)] for c in range(2)] for i in part]
-        ahead = [times(one[0][0], one[1][0]) for one in pair]
-        back = [times(one[1][1], one[0][1]) for one in pair]
-        cross = [split(times(one[0][0], one[1][2])) for one in pair]
-        cross = [times(x, one[0][1]) for x, one in zip(cross, pair)]
-        for at, i in enumerate(part):
-            s.chip_maps[i, 0] = ahead[at]
-            s.chip_maps[i, 1] = back[at]
-            s.chip_maps[i, 2] = s.both[0, half * core + i, 2] + cross[at]
-        for i in part:
-            send_map(i, True)
-
-            @pl.when(half * core + i == chip)
-            def _():
-                s.own_maps[chip] = s.chip_maps[i]
-
-    for copy in fetch[4:]:
-        copy.wait()
-    slab_matrices(s, number_ref)
+    for at in range(0, mode_dev, half):
+        last_maps(s, core, range(at, at + half), first, mode_total)
 
     others = s.spec_in.at[pl.ds(0, mode_axis - 1)]
     pltpu.make_async_remote_copy(
@@ -358,8 +413,6 @@
         s.vec_send[m, 2:4, :] = offset[2 * m : 2 * m + 2]
     swap = remote(s.vec_send, s.mate_vecs, s.sem_pv.at[0], s.sem_pv.at[1], partner)
     swap.start()
-    for share in shares[1]:
-        share.wait()
     low = lax.broadcasted_iota(jnp.int32, (8, n), 0) < 2
 
     @pl.when(core == 0)
@@ -375,112 +428,98 @@
             tile = s.vec_send[m]
             s.chip_vecs[m] = jnp.where(low, tile, mul(tile, s.both[0, m, 1]))
 
-    def vector_copy(m):
-        return remote(
-            s.chip_vecs.at[m],
-            s.own_vecs.at[core, chip],
-            s.sem_cv_s.at[m],
-            s.sem_cv_r.at[core, chip],
-            2 * m + m // half,
-        )
-
+    is_owner = chip // half == core
     for m in range(mode_dev):
-
-        @pl.when(me != 2 * m + m // half)
+        to = 2 * m + m // half
+
+        @pl.when(me != to)
         def _():
-            vector_copy(m).start()
-
-        @pl.when(me == 2 * m + m // half)
+            remote(s.chip_vecs.at[m], s.own_vecs.at[me], s.sem_cv.at[0], s.sem_cv.at[1], to).start()
+
+        @pl.when(me == to)
         def _():
-            s.own_vecs[core, chip] = s.chip_vecs[m]
-
-    owner = chip // half == core
-
-    @pl.when(owner)
-    def _():
-        for z in range(chips):
-            for c in range(2):
-
-                @pl.when(2 * z + c != me)
-                def _():
-                    remote(
-                        s.chip_vecs.at[0], s.own_vecs.at[c, z], s.sem_cv_s.at[0], s.sem_cv_r.at[c, z], me
-                    ).wait_recv()
-
+            s.own_vecs[me] = s.chip_vecs[m]
+
+    def tiles(ref, number, sems):
+        block = ref.at[pl.ds(0, number)]
+        return remote(block, block, sems.at[0], sems.at[1], me)
+
+    local_values = [None] * slabs
+    local_values[-1] = local[-1]
+    for j in reversed(range(slabs - 1)):
+        local_values[j] = local[j] - per_mode(banded(local_values[j + 1], s.es.at[j]), s.pts, j)
+    swap.wait()
+
+    @pl.when(core == 0)
+    def _():
+        for m in range(mode_dev):
+            turned = s.mate_vecs[m] + pltpu.roll(mul(s.vec_send[m], s.both[1, m, 2]), 2, 0)
+            s.fin[m] = pltpu.roll(turned, 6, 0)
+
+    @pl.when(core == 1)
+    def _():
+        s.fin[...] = s.mate_vecs[...]
+
+    within = jnp.concatenate([s.fin[m, 0:2, :] for m in range(mode_dev)], axis=0)
+    for j in range(slabs):
+        local_values[j] = local_values[j] + per_mode(within, s.extra, j)
+
+    @pl.when(is_owner)
+    def _():
+        tiles(s.own_vecs, count - 1, s.sem_cv).wait_recv()
+
+        def arrived(z, k):
             @pl.when(z != chip)
             def _():
-                two = pl.ds(0, 2)
-                if 0 < z < chips - 1:
-                    remote(
-                        s.chip_maps.at[0, two], s.own_maps.at[z, two], s.sem_cm_s.at[0, 0], s.sem_cm_r.at[z, 0], me
-                    ).wait_recv()
-                if z > 0:
-                    remote(
-                        s.chip_maps.at[0, 2], s.own_maps.at[z, 2], s.sem_cm_s.at[0, 1], s.sem_cm_r.at[z, 1], me
-                    ).wait_recv()
-
-        vecs = [s.own_vecs[0, z] + s.own_vecs[1, z] for z in range(chips)]
+                remote(
+                    s.chip_maps.at[0, k], s.own_maps.at[z, k], s.sem_cm_s.at[0, k], s.sem_cm_r.at[z, k], me
+                ).wait_recv()
+
+        for z in range(1, chips - 1):
+            arrived(z, 0)
+        vecs = [s.own_vecs[2 * z] + s.own_vecs[2 * z + 1] for z in range(chips)]
         state = jnp.zeros((8, n), F32)
         before = []
-        terms = []
         for z in range(chips):
             before.append(state)
-            if z > 0:
-                terms.append(vecs[z] + pltpu.roll(mul(state, s.own_maps[z, 2]), 2, 0))
-                if z < chips - 1:
-                    state = mul(state, s.own_maps[z, 0]) + vecs[z]
-            else:
-                terms.append(vecs[z])
+            if z == 0:
                 state = vecs[z]
+            elif z < chips - 1:
+                state = mul(state, s.own_maps[z, 0]) + vecs[z]
+        for z in range(1, chips):
+            arrived(z, 2)
+            if z < chips - 1:
+                arrived(z, 1)
+        terms = [vecs[0]]
+        for z in range(1, chips):
+            terms.append(vecs[z] + pltpu.roll(mul(before[z], s.own_maps[z, 2]), 2, 0))
         state = jnp.zeros((8, n), F32)
         for z in reversed(range(chips)):
-            s.back_send[z] = jnp.where(low, before[z], state)
-            for c in range(2):
-
-                @pl.when(2 * z + c != me)
-                def _():
-                    remote(
-                        s.back_send.at[z],
-                        s.back_vecs.at[chip],
-                        s.sem_bk_s.at[z, c],
-                        s.sem_bk_r.at[chip],
-                        2 * z + c,
-                    ).start()
-
-            @pl.when(z == chip)
-            def _():
-                s.back_vecs[chip] = s.back_send[z]
-
+            back = jnp.where(low, before[z], state)
+            s.back_send[2 * z] = back
+            s.back_send[2 * z + 1] = back
             if z > 0:
                 state = terms[z] if z == chips - 1 else mul(state, s.own_maps[z, 1]) + terms[z]
 
-    swap.wait()
-    for m in range(mode_dev):
-
-        @pl.when(me != 2 * m + m // half)
-        def _():
-            remote(s.back_send.at[0], s.back_vecs.at[m], s.sem_bk_s.at[0, 0], s.sem_bk_r.at[m], me).wait_recv()
-
-    @pl.when(core == 0)
-    def _():
-        for m in range(mode_dev):
-            ends = s.back_vecs[m]
-            middle = mul(ends, s.both[0, m, 0]) + s.vec_send[m]
-            turned = mul(ends, s.both[1, m, 1]) + s.mate_vecs[m]
-            s.fin[m] = jnp.where(low, ends, turned + pltpu.roll(mul(middle, s.both[1, m, 2]), 2, 0))
-
-    @pl.when(core == 1)
-    def _():
-        for m in range(mode_dev):
-            ends = s.back_vecs[m]
-            s.fin[m] = jnp.where(low, mul(ends, s.both[0, m, 0]) + s.mate_vecs[m], ends)
-
-    start = jnp.concatenate([s.fin[m, 0:2, :] for m in range(mode_dev)], axis=0)
-    end = jnp.concatenate([s.fin[m, 2:4, :] for m in range(mode_dev)], axis=0)
+        def answer(k, carry):
+            to = lax.rem(me + k, count)
+            remote(s.back_send.at[to], s.back_vecs.at[chip], s.sem_bk.at[0], s.sem_bk.at[1], to).start()
+            return carry
+
+        lax.fori_loop(1, count, answer, 0, unroll=True)
+        s.back_vecs[chip] = s.back_send[me]
+        tiles(s.back_vecs, mode_dev - 1, s.sem_bk).wait_recv()
+
+    @pl.when(jnp.logical_not(is_owner))
+    def _():
+        tiles(s.back_vecs, mode_dev, s.sem_bk).wait_recv()
+
+    start = jnp.concatenate([s.back_vecs[m, 0:2, :] for m in range(mode_dev)], axis=0)
+    end = jnp.concatenate([s.back_vecs[m, 2:4, :] for m in range(mode_dev)], axis=0)
+    bounds = jnp.concatenate([start, end], axis=1)
     values = [None] * slabs
     for j in reversed(range(slabs)):
-        full = local[j] + per_mode(start, s.nts, j)
-        values[j] = full - per_mode(end, s.pts, j)
+        values[j] = local_values[j] + per_mode(bounds, s.last, j)
         if j == slabs - 1:
             s.x_send[...] = values[j]
 
@@ -488,11 +527,19 @@
             def _():
                 remote(s.x_send, s.x_in, s.sem_x.at[0], s.sem_x.at[1], me + 1).start()
 
-        if j > 0:
-            end = banded(values[j], s.es.at[j - 1])
-
     for j in reversed(range(slabs)):
         if j == 0:
+            for i in range(half):
+                for k in range(3):
+                    send_map(i, k, False)
+
+            @pl.when(is_owner)
+            def _():
+                tiles(s.chip_vecs, mode_dev - 1, s.sem_cv).wait_send()
+
+            @pl.when(jnp.logical_not(is_owner))
+            def _():
+                tiles(s.chip_vecs, mode_dev, s.sem_cv).wait_send()
 
             @pl.when(me == 0)
             def _():
@@ -535,28 +582,9 @@
     def _():
         remote(s.x_send, s.x_in, s.sem_x.at[0], s.sem_x.at[1], me + 1).wait_send()
 
-    for i in range(half):
-        send_map(i, False)
-    for m in range(mode_dev):
-
-        @pl.when(me != 2 * m + m // half)
-        def _():
-            vector_copy(m).wait_send()
-
-    @pl.when(owner)
-    def _():
-        for z in range(chips):
-            for c in range(2):
-
-                @pl.when(2 * z + c != me)
-                def _():
-                    remote(
-                        s.back_send.at[z],
-                        s.back_vecs.at[chip],
-                        s.sem_bk_s.at[z, c],
-                        s.sem_bk_r.at[chip],
-                        2 * z + c,
-                    ).wait_send()
+    @pl.when(is_owner)
+    def _():
+        tiles(s.back_send, count - 1, s.sem_bk).wait_send()
 
 
 def fourier_table(planes):
@@ -592,7 +620,8 @@
     mode_total = mode_dev * mode_axis
     rows = 2 * mode_dev
     half = mode_dev // 2
-    parts = half // max(half // 2, 1)
+    parts = half
+    count = 2 * chips
     width = rhs_phys.shape[1]
 
     table = fourier_table(planes)
@@ -617,6 +646,8 @@
         pts=V(mode_dev, slabs, 2, n, n, dtype=BF16),
         uts=V(mode_dev, slabs, 2, n, n, dtype=BF16),
         nts=V(mode_dev, slabs, 2, n, n, dtype=BF16),
+        last=V(mode_dev, slabs, 2, 2 * n, n, dtype=BF16),
+        extra=V(mode_dev, slabs, 2, n, n, dtype=BF16),
         spec_out=V(mode_axis, rows, width),
         spec_in=V(mode_axis, rows, width),
         placed_in=V(rows, n),
@@ -629,22 +660,21 @@
         vec_send=V(mode_dev, 8, n),
         mate_vecs=V(mode_dev, 8, n),
         chip_vecs=V(mode_dev, 8, n),
-        own_vecs=V(2, chips, 8, n),
-        back_send=V(chips, 8, n),
+        own_vecs=V(count, 8, n),
+        back_send=V(count, 8, n),
         back_vecs=V(mode_dev, 8, n),
         fin=V(mode_dev, 8, n),
-        sem_in=D(len(LOADED)),
+        sem_in=D(len(LOADED) - 1),
+        sem_pa=D(parts, 2),
         sem_sp=D(2),
         sem_pm_s=D(2, parts),
         sem_pm_r=D(2, parts),
-        sem_cm_s=D(half, 2),
-        sem_cm_r=D(chips, 2),
+        sem_cm_s=D(half, 3),
+        sem_cm_r=D(chips, 3),
         sem_pl=D(2),
         sem_pv=D(2),
-        sem_cv_s=D(mode_dev),
-        sem_cv_r=D(2, chips),
-        sem_bk_s=D(chips, 2),
-        sem_bk_r=D(mode_dev),
+        sem_cv=D(2),
+        sem_bk=D(2),
         sem_x=D(2),
     )
     names = [name + "_hbm" for name in LOADED] + ["out"] + list(scratch)

time: 56.1 us -> 53.2 us (0.948)
  Pallas kernels: 54.2 us -> 51.4 us
    pallas_call x1, Pallas kernels: 54.2 us -> 51.4 us  [body(): pl.pallas_call(functools.partial(solve_kernel, names, mode_axis, mode_dev...]
where the time goes in v4:
time: 53.2 us; the launch traced here: 53 us
  Pallas kernels  51.4 us (97%)
  local copies, waits for them, and re-layouts  1.62 us (3%)
    pallas_call x1, Pallas kernels, body(): pl.pallas_call(functools.partial(solve_kernel, names, mode_axis, mode_dev...  51.4 us
    unnamed x1, local copies, waits for them, and re-layouts  1.62 us

profile of v4, /device:TPU:1, one launch (start us, length us, event | category | flops | bytes accessed | tf_op | source)
XLA Modules:
  0.0 53.0 jit_solution(3077530116077491232)
XLA Ops:
  0.0 51.4 %pressure_solve.1 = f32[16,3072]{1,0:T(8,128)} custom-call(f32[3,7,7]{2,1,0:T(8,128)} %axial_ref.1, f32[3,2,7]{2,1,0:T(2,128)} %couple_ref.1, f32[3,7]{1,0:T(4,128)} %axial_eig_ref.1, f32[3,128]{1,0:T(4,128)} %radial_eig_ref.1, s32[3,2,128]{2,1,0:T(2,128)} %number_ref.1, f32[8,3,128,128]{3,2,1,0:T(8,128)} %refs_0_.1, f32[2,3,128,128]{3,2,1,0:T(8,128)} %refs_1_.1, ...), custom_call_target="tpu_custom_call" | custom-call | tf_op jit(solution)/shard_map/pressure_solve/pallas_call | solution.py:681
  51.4 1.6 %copy.14 = f32[16,3072]{1,0:T(8,128)} copy(f32[16,3072]{1,0:T(8,128)} %pressure_solve.1) | data formatting | bytes 393216

commit v5 on v4

--- a/solution.py
+++ b/solution.py
@@ -194,20 +194,23 @@
     other = 1 - core
     partner = 2 * chip + other
 
-    parts = [[lax.rem(chip + k, half)] for k in range(half)]
+
+    def turn(k):
+        return lax.rem(chip + k, half)
+
+    def panel_copy(k, side):
+        block = pl.ds(half * jnp.where(side == 0, other, core) + turn(k), 1)
+        return pltpu.make_async_copy(s.panel_hbm.at[block], s.panel.at[block], s.sem_pa.at[k, side])
+
     fetch = {}
     for at, name in enumerate(LOADED[1:]):
         copy = pltpu.make_async_copy(getattr(s, name + "_hbm"), getattr(s, name), s.sem_in.at[at])
         copy.start()
         fetch[name] = copy
         if at == 0:
-            panels = []
-            for k, part in enumerate(parts):
-                for j, whose in enumerate((other, core)):
-                    block = pl.ds(half * whose + part[0], len(part))
-                    copy = pltpu.make_async_copy(s.panel_hbm.at[block], s.panel.at[block], s.sem_pa.at[k, j])
-                    copy.start()
-                    panels.append(copy)
+            for k in range(half):
+                for side in range(2):
+                    panel_copy(k, side).start()
 
     barrier = pltpu.get_barrier_semaphore()
     line = lax.axis_index("mode")
@@ -260,42 +263,46 @@
             )
             copy.start() if start else copy.wait_send()
 
-    def pairing(part, share):
-        share.wait()
-        pair = [[[split(s.both[c, half * core + i, k]) for k in range(3)] for c in range(2)] for i in part]
-        ahead = [times(one[0][0], one[1][0]) for one in pair]
-        back = [times(one[1][1], one[0][1]) for one in pair]
-        cross = [split(times(one[0][0], one[1][2])) for one in pair]
-        cross = [times(x, one[0][1]) for x, one in zip(cross, pair)]
-        for at, i in enumerate(part):
-            s.chip_maps[i, 0] = ahead[at]
-            s.chip_maps[i, 1] = back[at]
-            s.chip_maps[i, 2] = s.both[0, half * core + i, 2] + cross[at]
-        for i in part:
-            for k in (0, 2, 1):
-                send_map(i, k, True)
-
-            @pl.when(half * core + i == chip)
-            def _():
-                s.own_maps[chip] = s.chip_maps[i]
+    def share_copy(k, taken):
+        block = s.both.at[core, pl.ds(half * jnp.where(taken == 0, other, core) + turn(k), 1)]
+        return remote(block, block, s.sem_pm_s.at[taken, k], s.sem_pm_r.at[taken, k], partner)
+
+    def pairing(k):
+        share_copy(k, 0).wait()
+        i = turn(k)
+        one, two = ([split(s.both[c, half * core + i, k]) for k in range(3)] for c in range(2))
+        s.chip_maps[i, 0] = times(one[0], two[0])
+        s.chip_maps[i, 1] = times(two[1], one[1])
+        s.chip_maps[i, 2] = s.both[0, half * core + i, 2] + times(split(times(one[0], two[2])), one[1])
+        for k in (0, 2, 1):
+            send_map(i, k, True)
+
+        @pl.when(half * core + i == chip)
+        def _():
+            s.own_maps[chip] = s.chip_maps[i]
 
     fetch["band"].wait()
     first = line * mode_dev
-    shares = [[], []]
-    for at, part in enumerate(parts):
-        modes = [half * other + i for i in part] + [half * core + i for i in part]
-        for copy in panels[2 * at : 2 * at + 2]:
-            copy.wait()
-        mode_maps(s, core, modes, first, mode_total)
-        if at == 0:
+
+    def part_step(k, carry):
+        panel_copy(k, 0).wait()
+        panel_copy(k, 1).wait()
+        mode_maps(s, core, [half * other + turn(k), half * core + turn(k)], first, mode_total)
+
+        @pl.when(k == 0)
+        def _():
             pl.semaphore_wait(barrier, mode_axis - 1 + count - 1)
-        for whose, taken in ((other, 0), (core, 1)):
-            block = s.both.at[core, pl.ds(half * whose + part[0], len(part))]
-            share = remote(block, block, s.sem_pm_s.at[taken, at], s.sem_pm_r.at[taken, at], partner)
-            share.start()
-            shares[taken].append(share)
-        if at > 0:
-            pairing(parts[at - 1], shares[0][at - 1])
+
+        share_copy(k, 0).start()
+        share_copy(k, 1).start()
+
+        @pl.when(k > 0)
+        def _():
+            pairing(k - 1)
+
+        return carry
+
+    lax.fori_loop(0, half, part_step, 0)
 
     fetch["rhs"].wait()
     fetch["table"].wait()
@@ -318,15 +325,18 @@
     lax.fori_loop(1, mode_axis, spread_out, 0)
     s.spec_in[line] = s.spec_out[line]
 
-    pairing(parts[-1], shares[0][-1])
+    pairing(half - 1)
     for name in ("radial", "stiff", "mass"):
         fetch[name].wait()
     slab_matrices(s, number_ref)
 
-    for share in shares[1]:
-        share.wait()
-    for at in range(0, mode_dev, half):
-        last_maps(s, core, range(at, at + half), first, mode_total)
+    for k in range(half):
+        share_copy(k, 1).wait()
+
+    def last_step(at):
+        last_maps(s, core, [at * half + i for i in range(half)], first, mode_total)
+
+    last_step(0)
 
     others = s.spec_in.at[pl.ds(0, mode_axis - 1)]
     pltpu.make_async_remote_copy(
@@ -443,6 +453,8 @@
     def tiles(ref, number, sems):
         block = ref.at[pl.ds(0, number)]
         return remote(block, block, sems.at[0], sems.at[1], me)
+
+    last_step(1)
 
     local_values = [None] * slabs
     local_values[-1] = local[-1]

time: 53.2 us -> 53.1 us (level)
  no operation moved by 1% of the time
where the time goes in v5:
time: 53.1 us; the launch traced here: 52.9 us
  Pallas kernels  51.3 us (97%)
  local copies, waits for them, and re-layouts  1.62 us (3%)
    pallas_call x1, Pallas kernels, body(): pl.pallas_call(functools.partial(solve_kernel, names, mode_axis, mode_dev...  51.3 us
    unnamed x1, local copies, waits for them, and re-layouts  1.62 us

profile of v5, /device:TPU:1, one launch (start us, length us, event | category | flops | bytes accessed | tf_op | source)
XLA Modules:
  0.0 52.9 jit_solution(5220491241783369135)
XLA Ops:
  0.0 51.3 %pressure_solve.1 = f32[16,3072]{1,0:T(8,128)} custom-call(f32[3,7,7]{2,1,0:T(8,128)} %axial_ref.1, f32[3,2,7]{2,1,0:T(2,128)} %couple_ref.1, f32[3,7]{1,0:T(4,128)} %axial_eig_ref.1, f32[3,128]{1,0:T(4,128)} %radial_eig_ref.1, s32[3,2,128]{2,1,0:T(2,128)} %number_ref.1, f32[8,3,128,128]{3,2,1,0:T(8,128)} %refs_0_.1, f32[2,3,128,128]{3,2,1,0:T(8,128)} %refs_1_.1, ...), custom_call_target="tpu_custom_call" | custom-call | tf_op jit(solution)/shard_map/pressure_solve/pallas_call | solution.py:693
  51.3 1.6 %copy.14 = f32[16,3072]{1,0:T(8,128)} copy(f32[16,3072]{1,0:T(8,128)} %pressure_solve.1) | data formatting | bytes 393216

commit v6 on v4

--- a/solution.py
+++ b/solution.py
@@ -30,6 +30,10 @@
 
 def mul_split(v, hi, lo):
     vh, vl = split(v)
+    rows = v.shape[0]
+    if rows <= 16:
+        both = bdot(jnp.concatenate([vh, vl], axis=0), hi)
+        return both[:rows] + (both[rows:] + bdot(vh, lo))
     return bdot(vh, hi) + (bdot(vl, hi) + bdot(vh, lo))
 
 
@@ -528,6 +532,7 @@
                 remote(s.x_send, s.x_in, s.sem_x.at[0], s.sem_x.at[1], me + 1).start()
 
     for j in reversed(range(slabs)):
+        right = banded(values[j], s.lift.at[j, 1])
         if j == 0:
             for i in range(half):
                 for k in range(3):
@@ -549,10 +554,10 @@
             def _():
                 remote(s.x_send, s.x_in, s.sem_x.at[0], s.sem_x.at[1], me).wait_recv()
 
-            faces = [s.x_in[...], values[0]]
+            left_face = s.x_in[...]
         else:
-            faces = [values[j - 1], values[j]]
-        lifted = [banded(faces[side], s.lift.at[j, side]) for side in range(2)]
+            left_face = values[j - 1]
+        lifted = [banded(left_face, s.lift.at[j, 0]), right]
         spread = [
             lifted[0] * couple_ref[j, 0, a] + lifted[1] * couple_ref[j, 1, a] for a in range(inner)
         ]

time: 53.2 us -> 53 us (level)
  no operation moved by 1% of the time
where the time goes in v6:
time: 53 us; the launch traced here: 52.8 us
  Pallas kernels  51.1 us (96%)
  local copies, waits for them, and re-layouts  1.62 us (3%)
    pallas_call x1, Pallas kernels, body(): pl.pallas_call(functools.partial(solve_kernel, names, mode_axis, mode_dev...  51.1 us
    unnamed x1, local copies, waits for them, and re-layouts  1.62 us

profile of v6, /device:TPU:1, one launch (start us, length us, event | category | flops | bytes accessed | tf_op | source)
XLA Modules:
  0.0 52.8 jit_solution(7529789754149437433)
XLA Ops:
  0.0 51.1 %pressure_solve.1 = f32[16,3072]{1,0:T(8,128)} custom-call(f32[3,7,7]{2,1,0:T(8,128)} %axial_ref.1, f32[3,2,7]{2,1,0:T(2,128)} %couple_ref.1, f32[3,7]{1,0:T(4,128)} %axial_eig_ref.1, f32[3,128]{1,0:T(4,128)} %radial_eig_ref.1, s32[3,2,128]{2,1,0:T(2,128)} %number_ref.1, f32[8,3,128,128]{3,2,1,0:T(8,128)} %refs_0_.1, f32[2,3,128,128]{3,2,1,0:T(8,128)} %refs_1_.1, ...), custom_call_target="tpu_custom_call" | custom-call | tf_op jit(solution)/shard_map/pressure_solve/pallas_call | solution.py:686
  51.1 1.6 %copy.14 = f32[16,3072]{1,0:T(8,128)} copy(f32[16,3072]{1,0:T(8,128)} %pressure_solve.1) | data formatting | bytes 393216
